TPU v7x, 32 devices: a whole 2x2x4 slice. The times are simulated.
32 devices in a mesh: group: 2 (over y), clip: 4 (over x, core), seq: 4 (over z).
Axes of the slice: x: 2, y: 2, z: 4, core: 2. Of those that a mesh axis runs over, the one named last changes fastest.
Arguments:
- queries: bfloat16 [8, 512, 2048], P(('group', 'clip'), 'seq'), parts along dimension 0, may hold values from -18 to 18
- key_states: bfloat16 [8, 512, 2048], P(('group', 'clip'), 'seq'), parts along dimension 0, may hold values from -18 to 18
- value_states: bfloat16 [8, 512, 2048], P(('group', 'clip'), 'seq'), parts along dimension 0, may hold values from -6 to 6
- query_tangent: bfloat16 [8, 512, 2048], P(('group', 'clip'), 'seq'), parts along dimension 0, may hold values from -6 to 6
- key_tangent: bfloat16 [8, 512, 2048], P(('group', 'clip'), 'seq'), parts along dimension 0, may hold values from -6 to 6
- value_tangent: bfloat16 [8, 512, 2048], P(('group', 'clip'), 'seq'), parts along dimension 0, may hold values from -6 to 6
- offsets: int32 [8], P(('group', 'clip')), parts along dimension 0, may hold values from 0 to 130560
Outputs:
- attended: bfloat16 [8, 512, 2048], P(('group', 'clip'), 'seq'), parts along dimension 0
- attended_tangent: bfloat16 [8, 512, 2048], P(('group', 'clip'), 'seq'), parts along dimension 0
There are 2 independent parts, one for each index of `group`. A program takes and returns all parts, laid end to end along the dimension named above; each array names one. Nothing has to cross between parts.
All inputs are finite; a program needn't handle non-finite values.
Results may differ from a plain program's by a relative error of at most 0.012.
The roundings to bfloat16 on the way count: a program that leaves them out, or rounds other values in their place, can miss the bound.
Values may be sent and summed in bfloat16 or wider, within the bound.
No kernel may reach another device: no remote copies, remote signals or barrier semaphores. Data moves between devices by JAX's collectives and lax.ppermute only.
A program may use at most 64 MiB of HBM per device.

v0:
```python
import functools
import math

import jax
import jax.numpy as jnp
from jax import lax
from jax.experimental import pallas as pl
from jax.experimental.pallas import tpu as pltpu
from jax.sharding import PartitionSpec as P


H = 16
HD = 128
HH = 44
WW = 80


rope_theta = 10000.0

SIZES = (2, 2)
ORDERS = {'v': (2, 3, 1), 'qk': (1, 2, 3), 'out': (3, 2, 1)}


def rope_tables(first, count):
    global_index = first + jnp.arange(count, dtype=jnp.int32)
    frames = global_index // (HH * WW)
    grid_row = global_index // WW % HH
    column = global_index % WW
    spatial = HD // 6 * 2
    temporal = HD - 2 * spatial
    channel = jnp.arange(HD, dtype=jnp.int32)
    part_start = jnp.where(
        channel < temporal, 0, jnp.where(channel < temporal + spatial, temporal, temporal + spatial)
    )
    extent = jnp.where(channel < temporal, temporal, spatial)
    pair_index = (channel - part_start) // 2
    frequency = jnp.exp(
        -(2.0 * pair_index.astype(jnp.float32) / extent.astype(jnp.float32)) * math.log(rope_theta)
    )
    position = jnp.where(
        channel[None, :] < temporal,
        frames[:, None],
        jnp.where(channel[None, :] < temporal + spatial, grid_row[:, None], column[:, None]),
    )
    angles = position.astype(jnp.float32) * frequency[None, :]
    return (jnp.cos(angles), jnp.sin(angles))


def pack_values(value, vdot, wanted, tokens, width):
    count = sum(len(arrays) for _, arrays in wanted)

    def kernel(v_ref, vdot_ref, *rest):
        outs, sems = rest[:-1], rest[-1]
        me = lax.axis_index("seq")
        copies = []
        for out, (x, arrays) in zip(outs, wanted):
            columns = pl.ds(pl.multiple_of(jnp.bitwise_xor(me, x) * width, width), width)
            for i, a in enumerate(arrays):
                copies.append(
                    pltpu.make_async_copy(
                        (v_ref, vdot_ref)[a].at[0, :, columns], out.at[i], sems.at[len(copies)]
                    )
                )
        for copy in copies:
            copy.start()
        for copy in copies:
            copy.wait()

    return pl.pallas_call(
        kernel,
        out_shape=tuple(
            jax.ShapeDtypeStruct((len(arrays), tokens, width), jnp.bfloat16)
            for _, arrays in wanted
        ),
        in_specs=[pl.BlockSpec(memory_space=pltpu.HBM)] * 2,
        out_specs=tuple(pl.BlockSpec(memory_space=pltpu.VMEM) for _ in wanted),
        scratch_shapes=[pltpu.SemaphoreType.DMA((count,))],
        compiler_params=pltpu.CompilerParams(vmem_limit_bytes=8 << 20),
        cost_estimate=pl.CostEstimate(
            flops=0, bytes_accessed=4 * count * tokens * width, transcendentals=0
        ),
        name="pack_values",
    )(value, vdot)


def rope_kernel(blk_ref, q_ref, k_ref, qd_ref, kd_ref, cos_ref, sin_ref, *outs, n, sizes):
    step = pl.program_id(0)
    cosine = cos_ref[...]
    sine = sin_ref[...]
    lane = lax.broadcasted_iota(jnp.int32, cosine.shape, 1)
    even = lane % 2 == 0
    sine_signed = jnp.where(even, -sine, sine)
    for x in range(n):

        @pl.when(step == x)
        def _(x=x):
            for a, ref in enumerate((q_ref, k_ref, qd_ref, kd_ref)):
                for c, heads in enumerate(sizes):
                    for j in range(heads):
                        at = (sum(sizes[:c]) + j) * HD
                        t = ref[0, :, at : at + HD].astype(jnp.float32)
                        partner = jnp.where(
                            even, pltpu.roll(t, HD - 1, 1), pltpu.roll(t, 1, 1)
                        )
                        y = t * cosine + partner * sine_signed
                        outs[c * n + x][a, :, j * HD : (j + 1) * HD] = y.astype(jnp.bfloat16)


def rope_packs(blocks, q, k, qd, kd, cosine, sine, n, sizes):
    tokens = q.shape[1]
    width = sum(sizes) * HD
    column = pl.BlockSpec((1, tokens, width), lambda i, blk: (0, 0, blk[i]))
    table = pl.BlockSpec((tokens, HD), lambda i, blk: (0, 0))
    shapes = [(4, tokens, heads * HD) for heads in sizes for _ in range(n)]
    return pl.pallas_call(
        functools.partial(rope_kernel, n=n, sizes=sizes),
        out_shape=tuple(jax.ShapeDtypeStruct(shape, jnp.bfloat16) for shape in shapes),
        grid_spec=pltpu.PrefetchScalarGridSpec(
            num_scalar_prefetch=1,
            grid=(n,),
            in_specs=[column] * 4 + [table] * 2,
            out_specs=tuple(pl.BlockSpec(shape, lambda i, blk: (0, 0, 0)) for shape in shapes),
        ),
        compiler_params=pltpu.CompilerParams(vmem_limit_bytes=24 << 20),
        cost_estimate=pl.CostEstimate(
            flops=4 * tokens * n * width * 6,
            bytes_accessed=16 * tokens * n * width,
            transcendentals=0,
        ),
        name="rope_packs",
    )(blocks, q, k, qd, kd, cosine, sine)


def attend_kernel(blk_ref, v_ref, vd_ref, *refs, n):
    scaling = 1.0 / math.sqrt(HD)
    packs = refs[:n]
    values = refs[n:-n]
    outs = refs[-n:]
    nt = (((1,), (1,)), ((), ()))

    def dot(a, b):
        return jnp.dot(a, b, preferred_element_type=jnp.float32)

    def dot_t(a, b):
        return lax.dot_general(a, b, nt, preferred_element_type=jnp.float32)

    keys = jnp.concatenate([p[1] for p in packs], axis=0)
    kdots = jnp.concatenate([p[3] for p in packs], axis=0)
    both = jnp.concatenate([keys, kdots], axis=1)
    rows = [v[i] for v in values for i in range(v.shape[0])]
    vals = jnp.concatenate([v_ref[0]] + rows[0::2], axis=0)
    vdots = jnp.concatenate([vd_ref[0]] + rows[1::2], axis=0)
    vboth = jnp.concatenate([vals, vdots], axis=1)
    for x in range(n):
        q = packs[x][0]
        qd = packs[x][2]
        raw = dot_t(q, keys)
        largest = jnp.max(raw, axis=-1, keepdims=True)
        expons = jnp.exp((raw - largest) * scaling)
        inverse = 1.0 / jnp.sum(expons, axis=-1, keepdims=True)
        weights = (expons * inverse).astype(jnp.bfloat16)
        scores_dot = dot_t(jnp.concatenate([qd, q], axis=1), both) * scaling
        product = weights.astype(jnp.float32) * scores_dot
        correction = jnp.sum(product, axis=-1, keepdims=True)
        mixed = dot(weights, vboth)
        out = mixed[:, :HD]
        tangent = mixed[:, HD:] + dot(product.astype(jnp.bfloat16), vals) - correction * out
        outs[x][0] = out.astype(jnp.bfloat16)
        outs[x][1] = tangent.astype(jnp.bfloat16)


def attend(blocks, value, vdot, packs, values, start, heads, n):
    tokens = value.shape[1]
    per_device = H // n
    own = pl.BlockSpec(
        (1, tokens, HD), lambda j, blk: (0, 0, blk[0] * per_device + start + j)
    )
    pack = pl.BlockSpec((4, tokens, HD), lambda j, blk: (0, 0, j))
    values = [array for arrays in values for array in arrays]
    others = [
        pl.BlockSpec((array.shape[0], tokens, HD), lambda j, blk: (0, 0, start + j))
        for array in values
    ]
    out = pl.BlockSpec((2, tokens, HD), lambda j, blk: (0, 0, j))
    pairs = (n * tokens) ** 2 * heads
    return pl.pallas_call(
        functools.partial(attend_kernel, n=n),
        out_shape=tuple(
            jax.ShapeDtypeStruct((2, tokens, heads * HD), jnp.bfloat16) for _ in range(n)
        ),
        grid_spec=pltpu.PrefetchScalarGridSpec(
            num_scalar_prefetch=1,
            grid=(heads,),
            in_specs=[own] * 2 + [pack] * n + others,
            out_specs=(out,) * n,
        ),
        compiler_params=pltpu.CompilerParams(vmem_limit_bytes=24 << 20),
        cost_estimate=pl.CostEstimate(
            flops=12 * pairs * HD,
            bytes_accessed=16 * n * tokens * heads * HD,
            transcendentals=pairs,
        ),
        name="attend",
    )(blocks, value, vdot, *packs, *values)


def place(pieces, width, tokens, into=None):
    shape = jax.ShapeDtypeStruct((1, tokens, H * HD), jnp.bfloat16)
    total = sum(piece.shape[2] for _, _, piece in pieces)

    def kernel(*refs):
        ins, outs, sems = refs[: len(pieces)], refs[-3:-1], refs[-1]
        me = lax.axis_index("seq")
        copies = []
        for ref, (x, column, _) in zip(ins, pieces):
            first = pl.multiple_of(jnp.bitwise_xor(me, x) * width + column, HD)
            for a in range(2):
                copies.append(
                    pltpu.make_async_copy(
                        ref.at[a],
                        outs[a].at[0, :, pl.ds(first, ref.shape[2])],
                        sems.at[len(copies)],
                    )
                )
        for copy in copies:
            copy.start()
        for copy in copies:
            copy.wait()

    into = () if into is None else tuple(into)
    return pl.pallas_call(
        kernel,
        out_shape=(shape, shape),
        in_specs=[pl.BlockSpec(memory_space=pltpu.VMEM)] * len(pieces)
        + [pl.BlockSpec(memory_space=pl.ANY)] * len(into),
        out_specs=(pl.BlockSpec(memory_space=pl.ANY),) * 2,
        scratch_shapes=[pltpu.SemaphoreType.DMA((2 * len(pieces),))],
        input_output_aliases={len(pieces) + i: i for i in range(len(into))},
        compiler_params=pltpu.CompilerParams(vmem_limit_bytes=8 << 20),
        cost_estimate=pl.CostEstimate(
            flops=0, bytes_accessed=8 * tokens * total, transcendentals=0
        ),
        name="place",
    )(*(piece for _, _, piece in pieces), *into)


def chunk_sizes(n):
    per_device = H // n
    return SIZES if per_device == 4 else (1,) * per_device


def partner_order(n, kind):
    middle_first = sorted(range(1, n), key=lambda x: (-x.bit_length(), x))
    return [x for x in ORDERS[kind] if x < n] if n == 4 else middle_first


def body_pairs(*args):
    return pairs_program(*args)


def pairs_program(queries, key_states, value_states, query_tangent, key_tangent, value_tangent, offsets):
    n = lax.axis_size("seq")
    order = partner_order(n, "v")
    sizes = chunk_sizes(n)
    starts = [sum(sizes[:c]) for c in range(len(sizes))]
    tokens = queries.shape[1]
    width = H // n * HD
    me = lax.axis_index("seq")
    value_hbm = pltpu.with_memory_space_constraint(value_states, pltpu.HBM)
    vdot_hbm = pltpu.with_memory_space_constraint(value_tangent, pltpu.HBM)

    def swap(array, x):
        return lax.ppermute(array, "seq", [(i, i ^ x) for i in range(n)])

    value_in = {}
    for xs in (order[:1], order[1:]):
        wanted = [(x, (0, 1)) for x in xs]
        if wanted:
            sent = pack_values(value_hbm, vdot_hbm, wanted, tokens, width)
            for x, array in zip(xs, sent):
                value_in[x] = (swap(array, x),)

    blocks = jnp.bitwise_xor(jnp.arange(n, dtype=jnp.int32), me.astype(jnp.int32))
    cosine, sine = rope_tables(offsets[0] + me * tokens, tokens)
    packs = rope_packs(
        blocks, queries, key_states, query_tangent, key_tangent, cosine, sine, n, sizes
    )
    packs_in = []
    for c in range(len(sizes)):
        mine = packs[c * n : (c + 1) * n]
        got = {x: swap(mine[x], x) for x in partner_order(n, "qk")}
        packs_in.append([mine[0]] + [got[x] for x in range(1, n)])
    early, late = [], []
    for c, (start, heads) in enumerate(zip(starts, sizes)):
        outs = attend(
            blocks,
            value_states,
            value_tangent,
            packs_in[c],
            [value_in[x] for x in range(1, n)],
            start,
            heads,
            n,
        )
        early.append((0, start * HD, outs[0]))
        last = early if c < len(sizes) - 1 else late
        last += [(x, start * HD, swap(outs[x], x)) for x in partner_order(n, "out")]
    placed = place(early, width, tokens)
    return place(late, width, tokens, placed)


def rotate(tensor, cosine, sine):
    channel = jnp.arange(tensor.shape[-1], dtype=jnp.int32)
    partner = jnp.where(
        channel % 2 == 0, -jnp.roll(tensor, -1, axis=-1), jnp.roll(tensor, 1, axis=-1)
    )
    return (tensor * cosine + partner * sine).astype(jnp.bfloat16)


def primal_terms(query_blk, keys_all, values_all, scaling):
    scores = (
        jnp.einsum("bhd,khd->hbk", query_blk, keys_all, preferred_element_type=jnp.float32)
        * scaling
    )
    largest = jnp.max(scores, axis=-1, keepdims=True)
    expons = jnp.exp(scores - largest)
    probs = expons / jnp.sum(expons, axis=-1, keepdims=True)
    weights = probs.astype(jnp.bfloat16)
    out_full = jnp.einsum("hbk,khd->bhd", weights, values_all, preferred_element_type=jnp.float32)
    return (weights, out_full)


def tangent_terms(
    query_blk, qdot_blk, keys_all, kdots_all, values_all, vdots_all, weights, out_full, scaling
):
    scores_dot = (
        jnp.einsum("bhd,khd->hbk", qdot_blk, keys_all, preferred_element_type=jnp.float32)
        + jnp.einsum("bhd,khd->hbk", query_blk, kdots_all, preferred_element_type=jnp.float32)
    ) * scaling
    product = weights.astype(jnp.float32) * scores_dot
    correction = jnp.sum(product, axis=-1)
    product_half = product.astype(jnp.bfloat16)
    tangent = (
        jnp.einsum("hbk,khd->bhd", weights, vdots_all, preferred_element_type=jnp.float32)
        + jnp.einsum("hbk,khd->bhd", product_half, values_all, preferred_element_type=jnp.float32)
        - jnp.transpose(correction)[:, :, None] * out_full
    )
    return tangent.astype(jnp.bfloat16)


def body_general(queries, key_states, value_states, query_tangent, key_tangent, value_tangent, offsets):
    devices = lax.axis_size("seq")
    repeat = max(devices // H, 1)
    per_device = max(H // devices, 1)
    groups = H // per_device
    width = per_device * HD
    tokens = queries.shape[1]
    sub_rows = tokens // repeat
    scaling = 1.0 / math.sqrt(HD)
    first = offsets[0] + lax.axis_index("seq") * tokens
    cosine, sine = (t[:, None, :] for t in rope_tables(first, tokens))

    def roped(array):
        return rotate(array[0].reshape(tokens, H, HD).astype(jnp.float32), cosine, sine).reshape(
            tokens, H * HD
        )

    def by_rows(array):
        shaped = array.reshape(repeat, sub_rows, groups, width)
        return jnp.transpose(shaped, (2, 0, 1, 3)).reshape(devices, sub_rows, width)

    def by_copies(array):
        shaped = jnp.transpose(array.reshape(tokens, groups, width), (1, 0, 2))
        spread = jnp.broadcast_to(shaped[:, None], (groups, repeat, tokens, width))
        return spread.reshape(devices, tokens, width)

    query_send = by_rows(roped(queries))
    qdot_send = by_rows(roped(query_tangent))
    key_send = by_copies(roped(key_states))
    kdot_send = by_copies(roped(key_tangent))
    value_send = by_copies(value_states[0])
    vdot_send = by_copies(value_tangent[0])
    query_rows = devices * sub_rows
    block = min(512, query_rows)
    count = query_rows // block

    def heads_view(array):
        return array.reshape(array.shape[0], per_device, HD)

    def blocks(array):
        return array.reshape(count, block, per_device, HD)

    received = (
        lax.all_to_all(query_send, "seq", split_axis=0, concat_axis=1, tiled=True),
        lax.all_to_all(key_send, "seq", split_axis=0, concat_axis=1, tiled=True),
        lax.all_to_all(value_send, "seq", split_axis=0, concat_axis=1, tiled=True),
        lax.all_to_all(qdot_send, "seq", split_axis=0, concat_axis=1, tiled=True),
        lax.all_to_all(kdot_send, "seq", split_axis=0, concat_axis=1, tiled=True),
        lax.all_to_all(vdot_send, "seq", split_axis=0, concat_axis=1, tiled=True),
    )
    query_in, key_in, value_in, qdot_in, kdot_in, vdot_in = tuple((array[0] for array in received))
    keys_all, values_all = (heads_view(key_in), heads_view(value_in))
    kdots_all, vdots_all = (heads_view(kdot_in), heads_view(vdot_in))

    def one_block(parts):
        query_blk, qdot_blk = parts
        weights, out_full = primal_terms(query_blk, keys_all, values_all, scaling)
        tangent = tangent_terms(
            query_blk,
            qdot_blk,
            keys_all,
            kdots_all,
            values_all,
            vdots_all,
            weights,
            out_full,
            scaling,
        )
        return (out_full.astype(jnp.bfloat16), tangent)

    attended, tangent_out = lax.map(one_block, (blocks(query_in), blocks(qdot_in)))

    def to_sources(array):
        return array.reshape(devices, sub_rows, width)

    returned = (
        lax.all_to_all(to_sources(attended), "seq", split_axis=0, concat_axis=0, tiled=True),
        lax.all_to_all(to_sources(tangent_out), "seq", split_axis=0, concat_axis=0, tiled=True),
    )

    def to_tokens(array):
        shaped = array.reshape(groups, repeat, sub_rows, width)
        return jnp.transpose(shaped, (1, 2, 0, 3)).reshape(tokens, H * HD)[None]

    return (to_tokens(returned[0]), to_tokens(returned[1]))


def solution(mesh):
    in_specs = (
        P(("group", "clip"), "seq", None),
        P(("group", "clip"), "seq", None),
        P(("group", "clip"), "seq", None),
        P(("group", "clip"), "seq", None),
        P(("group", "clip"), "seq", None),
        P(("group", "clip"), "seq", None),
        P(("group", "clip")),
    )
    out_specs = (P(("group", "clip"), "seq", None), P(("group", "clip"), "seq", None))
    n = mesh.shape["seq"]
    whole_heads = n > 1 and n & (n - 1) == 0 and H % n == 0
    body = body_pairs if whole_heads else body_general
    return jax.shard_map(body, mesh=mesh, in_specs=in_specs, out_specs=out_specs, check_vma=False)
```

profile of v0, /device:TPU:0, one launch (start us, length us, event | category | flops | bytes accessed | tf_op | source)
XLA Modules:
  0.0 97.3 jit_solution(15421259397648772927)
XLA Ops:
  0.6 0.0 copy-start.4
  0.6 0.0 copy-start.5
  0.6 1.1 %pack_values.3 = bf16[2,128,512]{2,1,0:T(8,128)(2,1)S(1)} custom-call(bf16[1,128,2048]{2,1,0:T(8,128)(2,1)} %v_ref.7, bf16[1,128,2048]{2,1,0:T(8,128)(2,1)} %vd_ref.3), custom_call_target="tpu_custom_call" | custom-call | bytes 524288 | tf_op jit(solution)/shard_map/pack_values/pallas_call | solution.py:69
  1.7 0.0 copy-start.2
  1.7 0.0 copy-start.3
  1.8 4.1 %collective-permute-start.4 = (bf16[2,128,512]{2,1,0:T(8,128)(2,1)S(1)}, bf16[2,128,512]{2,1,0:T(8,128)(2,1)S(1)}, u32[]{:S(2)}, u32[]{:S(2)}) collective-permute-start(bf16[2,128,512]{2,1,0:T(8,128)(2,1)S(1)} %pack_values.3), channel_id=1, source_target_pairs={{0,2},{1,3},{2,0},{3,1},{4,6},{5,7},{6,4},{7,5},{8,10},{9,11},{10,... | collective-permute-start | bytes 786440 | tf_op jit(solution)/shard_map/ppermute | solution.py:273
  5.9 1.8 %pack_values.2 = (bf16[2,128,512]{2,1,0:T(8,128)(2,1)S(1)}, bf16[2,128,512]{2,1,0:T(8,128)(2,1)}) custom-call(bf16[1,128,2048]{2,1,0:T(8,128)(2,1)} %v_ref.7, bf16[1,128,2048]{2,1,0:T(8,128)(2,1)} %vd_ref.3), custom_call_target="tpu_custom_call" | custom-call | bytes 1048576 | tf_op jit(solution)/shard_map/pack_values/pallas_call | solution.py:69
  7.7 1.6 %collective-permute-start.3 = (bf16[2,128,512]{2,1,0:T(8,128)(2,1)}, bf16[2,128,512]{2,1,0:T(8,128)(2,1)S(1)}, u32[]{:S(2)}, u32[]{:S(2)}) collective-permute-start(bf16[2,128,512]{2,1,0:T(8,128)(2,1)} %get-tuple-element.26), channel_id=1, source_target_pairs={{0,1},{1,0},{2,3},{3,2},{4,5},{5,4},{6,7},{7,6},{8,9},{9,8},{10,11... | collective-permute-start | bytes 786440 | tf_op jit(solution)/shard_map/ppermute | solution.py:273
  9.4 0.0 collective-permute-start.5
  10.1 0.3 fusion
  10.5 0.0 copy-done.4
  10.5 0.0 copy-done.5
  10.5 0.0 copy-done.2
  10.5 0.0 copy-done.3
  10.5 0.0 copy-start
  10.5 0.0 copy-start.1
  10.5 2.7 %rope_packs.1 = (bf16[4,128,256]{2,1,0:T(8,128)(2,1)S(1)}, bf16[4,128,256]{2,1,0:T(8,128)(2,1)S(1)}, bf16[4,128,256]{2,1,0:T(8,128)(2,1)S(1)}, bf16[4,128,256]{2...) custom-call(s32[4]{0:T(128)S(1)} %iota_xor_fusion.blk_ref, ...), custom_call_target="tpu_custom_call" | custom-call | flops 6291456 | bytes 4194304 | tf_op jit(solution)/shard_map/rope_packs/pallas_call | solution.py:115
  13.2 1.0 collective-permute-start.9
  14.2 3.5 %collective-permute-start.10 = (bf16[4,128,256]{2,1,0:T(8,128)(2,1)S(1)}, bf16[4,128,256]{2,1,0:T(8,128)(2,1)S(1)}, u32[]{:S(2)}, u32[]{:S(2)}) collective-permute-start(bf16[4,128,256]{2,1,0:T(8,128)(2,1)S(1)} %get-tuple-element.33), channel_id=1, source_target_pairs={{0,2},{1,3},{2,0},{3,1},{4,6},{5,7},{6,4},{7,5},{8,10},{9,11},{10,... | collective-permute-start | bytes 786440 | tf_op jit(solution)/shard_map/ppermute | solution.py:273
  17.7 1.9 %collective-permute-done.4.refs_5_ = bf16[2,128,512]{2,1,0:T(8,128)(2,1)S(1)} collective-permute-done((bf16[2,128,512]{2,1,0:T(8,128)(2,1)S(1)}, bf16[2,128,512]{2,1,0:T(8,128)(2,1)S(1)}, u32[]{:S(2)}, u32[]{:S(2)}) %collective-permute-start.4) | collective-permute-done | bytes 262176 | tf_op jit(solution)/shard_map/ppermute | solution.py:273
  19.6 3.0 %collective-permute-start.11 = (bf16[4,128,256]{2,1,0:T(8,128)(2,1)S(1)}, bf16[4,128,256]{2,1,0:T(8,128)(2,1)S(1)}, u32[]{:S(2)}, u32[]{:S(2)}) collective-permute-start(bf16[4,128,256]{2,1,0:T(8,128)(2,1)S(1)} %get-tuple-element.34), channel_id=1, source_target_pairs={{0,3},{1,2},{2,1},{3,0},{4,7},{5,6},{6,5},{7,4},{8,11},{9,10},{10,... | collective-permute-start | bytes 786440 | tf_op jit(solution)/shard_map/ppermute | solution.py:273
  22.6 4.6 %collective-permute-done.3.refs_4_ = bf16[2,128,512]{2,1,0:T(8,128)(2,1)S(1)} collective-permute-done((bf16[2,128,512]{2,1,0:T(8,128)(2,1)}, bf16[2,128,512]{2,1,0:T(8,128)(2,1)S(1)}, u32[]{:S(2)}, u32[]{:S(2)}) %collective-permute-start.3) | collective-permute-done | bytes 262176 | tf_op jit(solution)/shard_map/ppermute | solution.py:273
  27.3 0.0 collective-permute-start
  27.3 0.0 collective-permute-done.5.refs_6_
  27.3 5.7 %collective-permute-start.1 = (bf16[4,128,256]{2,1,0:T(8,128)(2,1)S(1)}, bf16[4,128,256]{2,1,0:T(8,128)(2,1)S(1)}, u32[]{:S(2)}, u32[]{:S(2)}) collective-permute-start(bf16[4,128,256]{2,1,0:T(8,128)(2,1)S(1)} %get-tuple-element.24), channel_id=1, source_target_pairs={{0,2},{1,3},{2,0},{3,1},{4,6},{5,7},{6,4},{7,5},{8,10},{9,11},{10,... | collective-permute-start | bytes 786440 | tf_op jit(solution)/shard_map/ppermute | solution.py:273
  33.0 1.1 %collective-permute-done.9.refs_1_ = bf16[4,128,256]{2,1,0:T(8,128)(2,1)S(1)} collective-permute-done((bf16[4,128,256]{2,1,0:T(8,128)(2,1)S(1)}, bf16[4,128,256]{2,1,0:T(8,128)(2,1)S(1)}, u32[]{:S(2)}, u32[]{:S(2)}) %collective-permute-start.9) | collective-permute-done | bytes 262176 | tf_op jit(solution)/shard_map/ppermute | solution.py:273
  34.1 1.3 %collective-permute-start.2 = (bf16[4,128,256]{2,1,0:T(8,128)(2,1)S(1)}, bf16[4,128,256]{2,1,0:T(8,128)(2,1)S(1)}, u32[]{:S(2)}, u32[]{:S(2)}) collective-permute-start(bf16[4,128,256]{2,1,0:T(8,128)(2,1)S(1)} %get-tuple-element.25), channel_id=1, source_target_pairs={{0,3},{1,2},{2,1},{3,0},{4,7},{5,6},{6,5},{7,4},{8,11},{9,10},{10,... | collective-permute-start | bytes 786440 | tf_op jit(solution)/shard_map/ppermute | solution.py:273
  35.3 12.3 %collective-permute-done.10.refs_2_ = bf16[4,128,256]{2,1,0:T(8,128)(2,1)S(1)} collective-permute-done((bf16[4,128,256]{2,1,0:T(8,128)(2,1)S(1)}, bf16[4,128,256]{2,1,0:T(8,128)(2,1)S(1)}, u32[]{:S(2)}, u32[]{:S(2)}) %collective-permute-start.10) | collective-permute-done | bytes 262176 | tf_op jit(solution)/shard_map/ppermute | solution.py:273
  47.6 0.0 collective-permute-done.11.refs_3_
  47.6 0.0 copy-done
  47.6 0.0 copy-done.1
  47.6 4.7 %attend.3 = (bf16[2,128,256]{2,1,0:T(8,128)(2,1)S(1)}, bf16[2,128,256]{2,1,0:T(8,128)(2,1)S(1)}, bf16[2,128,256]{2,1,0:T(8,128)(2,1)S(1)}, bf16[2,128,256]{2,1,0:T(8,128)(2,1)S(1)}) custom-call(s32[4]{0:T(128)S(1)} %iota_xor_fusion.blk_ref, bf16[1,128,2048]{2,1,0:T(8,128)(2,1)S(1)} %copy-done, bf16[1,128,2048]{2,1,0:T(8,128)(2,1)S(1)} %copy-done.1, ...), custom_call_target="tpu_custom_call" | custom-call | flops 805306368 | bytes 2097152 | tf_op jit(solution)/shard_map/attend/pallas_call | solution.py:186
  52.3 3.2 %collective-permute-start.12 = (bf16[2,128,256]{2,1,0:T(8,128)(2,1)S(1)}, bf16[2,128,256]{2,1,0:T(8,128)(2,1)S(1)}, u32[]{:S(2)}, u32[]{:S(2)}) collective-permute-start(bf16[2,128,256]{2,1,0:T(8,128)(2,1)S(1)} %get-tuple-element.36), channel_id=1, source_target_pairs={{0,3},{1,2},{2,1},{3,0},{4,7},{5,6},{6,5},{7,4},{8,11},{9,10},{10,... | collective-permute-start | bytes 393224 | tf_op jit(solution)/shard_map/ppermute | solution.py:273
  55.5 17.8 %collective-permute-start.13 = (bf16[2,128,256]{2,1,0:T(8,128)(2,1)S(1)}, bf16[2,128,256]{2,1,0:T(8,128)(2,1)S(1)}, u32[]{:S(2)}, u32[]{:S(2)}) collective-permute-start(bf16[2,128,256]{2,1,0:T(8,128)(2,1)S(1)} %get-tuple-element.37), channel_id=1, source_target_pairs={{0,2},{1,3},{2,0},{3,1},{4,6},{5,7},{6,4},{7,5},{8,10},{9,11},{10,... | collective-permute-start | bytes 393224 | tf_op jit(solution)/shard_map/ppermute | solution.py:273
  73.3 0.0 collective-permute-done.refs_1_
  73.3 0.4 collective-permute-start.14
  73.7 0.0 collective-permute-done.1.refs_2_
  73.7 0.0 collective-permute-done.2.refs_3_
  73.7 4.7 %attend.2 = (bf16[2,128,256]{2,1,0:T(8,128)(2,1)S(1)}, bf16[2,128,256]{2,1,0:T(8,128)(2,1)S(1)}, bf16[2,128,256]{2,1,0:T(8,128)(2,1)S(1)}, bf16[2,128,256]{2,1,0:T(8,128)(2,1)S(1)}) custom-call(s32[4]{0:T(128)S(1)} %iota_xor_fusion.blk_ref, bf16[1,128,2048]{2,1,0:T(8,128)(2,1)S(1)} %copy-done, bf16[1,128,2048]{2,1,0:T(8,128)(2,1)S(1)} %copy-done.1, ...), custom_call_target="tpu_custom_call" | custom-call | flops 805306368 | bytes 2097152 | tf_op jit(solution)/shard_map/attend/pallas_call | solution.py:186
  78.4 2.4 %collective-permute-start.6 = (bf16[2,128,256]{2,1,0:T(8,128)(2,1)S(1)}, bf16[2,128,256]{2,1,0:T(8,128)(2,1)S(1)}, u32[]{:S(2)}, u32[]{:S(2)}) collective-permute-start(bf16[2,128,256]{2,1,0:T(8,128)(2,1)S(1)} %get-tuple-element.28), channel_id=1, source_target_pairs={{0,3},{1,2},{2,1},{3,0},{4,7},{5,6},{6,5},{7,4},{8,11},{9,10},{10,... | collective-permute-start | bytes 393224 | tf_op jit(solution)/shard_map/ppermute | solution.py:273
  80.9 6.5 %collective-permute-start.7 = (bf16[2,128,256]{2,1,0:T(8,128)(2,1)S(1)}, bf16[2,128,256]{2,1,0:T(8,128)(2,1)S(1)}, u32[]{:S(2)}, u32[]{:S(2)}) collective-permute-start(bf16[2,128,256]{2,1,0:T(8,128)(2,1)S(1)} %get-tuple-element.29), channel_id=1, source_target_pairs={{0,2},{1,3},{2,0},{3,1},{4,6},{5,7},{6,4},{7,5},{8,10},{9,11},{10,... | collective-permute-start | bytes 393224 | tf_op jit(solution)/shard_map/ppermute | solution.py:273
  87.4 0.0 collective-permute-done.12.refs_1_
  87.4 0.4 collective-permute-start.8
  87.8 0.5 collective-permute-done.13.refs_2_
  88.3 0.0 collective-permute-done.14.refs_3_
  88.3 0.9 place.2
  89.2 0.0 collective-permute-done.6.refs_0_
  89.2 7.4 %collective-permute-done.7.refs_1_ = bf16[2,128,256]{2,1,0:T(8,128)(2,1)S(1)} collective-permute-done((bf16[2,128,256]{2,1,0:T(8,128)(2,1)S(1)}, bf16[2,128,256]{2,1,0:T(8,128)(2,1)S(1)}, u32[]{:S(2)}, u32[]{:S(2)}) %collective-permute-start.7) | collective-permute-done | bytes 131104 | tf_op jit(solution)/shard_map/ppermute | solution.py:273
  96.6 0.0 collective-permute-done.8.refs_2_
  96.6 0.8 place.3
  (5 shorter events, 0.1 us)
Async XLA Ops:
  0.6 9.8 %copy-start.4 = (bf16[1,128,2048]{2,1,0:T(8,128)(2,1)S(1)}, bf16[1,128,2048]{2,1,0:T(8,128)(2,1)}, u32[]{:S(2)}) copy-start(bf16[1,128,2048]{2,1,0:T(8,128)(2,1)} %qd_ref.1) | copy-start | bytes 1572868
  0.6 9.8 %copy-start.5 = (bf16[1,128,2048]{2,1,0:T(8,128)(2,1)S(1)}, bf16[1,128,2048]{2,1,0:T(8,128)(2,1)}, u32[]{:S(2)}) copy-start(bf16[1,128,2048]{2,1,0:T(8,128)(2,1)} %kd_ref.1) | copy-start | bytes 1572868
  1.7 8.8 %copy-start.2 = (bf16[1,128,2048]{2,1,0:T(8,128)(2,1)S(1)}, bf16[1,128,2048]{2,1,0:T(8,128)(2,1)}, u32[]{:S(2)}) copy-start(bf16[1,128,2048]{2,1,0:T(8,128)(2,1)} %q_ref.1) | copy-start | bytes 1572868
  1.7 8.8 %copy-start.3 = (bf16[1,128,2048]{2,1,0:T(8,128)(2,1)S(1)}, bf16[1,128,2048]{2,1,0:T(8,128)(2,1)}, u32[]{:S(2)}) copy-start(bf16[1,128,2048]{2,1,0:T(8,128)(2,1)} %k_ref.1) | copy-start | bytes 1572868
  1.8 17.8 %collective-permute-start.4 = (bf16[2,128,512]{2,1,0:T(8,128)(2,1)S(1)}, bf16[2,128,512]{2,1,0:T(8,128)(2,1)S(1)}, u32[]{:S(2)}, u32[]{:S(2)}) collective-permute-start(bf16[2,128,512]{2,1,0:T(8,128)(2,1)S(1)} %pack_values.3), channel_id=1, source_target_pairs={{0,2},{1,3},{2,0},{3,1},{4,6},{5,7},{6,4},{7,5},{8,10},{9,11},{10,... | collective-permute-start | bytes 786440 | tf_op jit(solution)/shard_map/ppermute | solution.py:273
  7.7 19.5 %collective-permute-start.3 = (bf16[2,128,512]{2,1,0:T(8,128)(2,1)}, bf16[2,128,512]{2,1,0:T(8,128)(2,1)S(1)}, u32[]{:S(2)}, u32[]{:S(2)}) collective-permute-start(bf16[2,128,512]{2,1,0:T(8,128)(2,1)} %get-tuple-element.26), channel_id=1, source_target_pairs={{0,1},{1,0},{2,3},{3,2},{4,5},{5,4},{6,7},{7,6},{8,9},{9,8},{10,11... | collective-permute-start | bytes 786440 | tf_op jit(solution)/shard_map/ppermute | solution.py:273
  9.4 17.9 %collective-permute-start.5 = (bf16[2,128,512]{2,1,0:T(8,128)(2,1)S(1)}, bf16[2,128,512]{2,1,0:T(8,128)(2,1)S(1)}, u32[]{:S(2)}, u32[]{:S(2)}) collective-permute-start(bf16[2,128,512]{2,1,0:T(8,128)(2,1)S(1)} %get-tuple-element.27), channel_id=1, source_target_pairs={{0,3},{1,2},{2,1},{3,0},{4,7},{5,6},{6,5},{7,4},{8,11},{9,10},{10,... | collective-permute-start | bytes 786440 | tf_op jit(solution)/shard_map/ppermute | solution.py:273
  10.5 37.1 %copy-start = (bf16[1,128,2048]{2,1,0:T(8,128)(2,1)S(1)}, bf16[1,128,2048]{2,1,0:T(8,128)(2,1)}, u32[]{:S(2)}) copy-start(bf16[1,128,2048]{2,1,0:T(8,128)(2,1)} %v_ref.7) | copy-start | bytes 1572868
  10.5 37.1 %copy-start.1 = (bf16[1,128,2048]{2,1,0:T(8,128)(2,1)S(1)}, bf16[1,128,2048]{2,1,0:T(8,128)(2,1)}, u32[]{:S(2)}) copy-start(bf16[1,128,2048]{2,1,0:T(8,128)(2,1)} %vd_ref.3) | copy-start | bytes 1572868
  13.2 20.8 %collective-permute-start.9 = (bf16[4,128,256]{2,1,0:T(8,128)(2,1)S(1)}, bf16[4,128,256]{2,1,0:T(8,128)(2,1)S(1)}, u32[]{:S(2)}, u32[]{:S(2)}) collective-permute-start(bf16[4,128,256]{2,1,0:T(8,128)(2,1)S(1)} %get-tuple-element.32), channel_id=1, source_target_pairs={{0,1},{1,0},{2,3},{3,2},{4,5},{5,4},{6,7},{7,6},{8,9},{9,8},{10,11... | collective-permute-start | bytes 786440 | tf_op jit(solution)/shard_map/ppermute | solution.py:273
  14.2 33.4 %collective-permute-start.10 = (bf16[4,128,256]{2,1,0:T(8,128)(2,1)S(1)}, bf16[4,128,256]{2,1,0:T(8,128)(2,1)S(1)}, u32[]{:S(2)}, u32[]{:S(2)}) collective-permute-start(bf16[4,128,256]{2,1,0:T(8,128)(2,1)S(1)} %get-tuple-element.33), channel_id=1, source_target_pairs={{0,2},{1,3},{2,0},{3,1},{4,6},{5,7},{6,4},{7,5},{8,10},{9,11},{10,... | collective-permute-start | bytes 786440 | tf_op jit(solution)/shard_map/ppermute | solution.py:273
  19.6 28.0 %collective-permute-start.11 = (bf16[4,128,256]{2,1,0:T(8,128)(2,1)S(1)}, bf16[4,128,256]{2,1,0:T(8,128)(2,1)S(1)}, u32[]{:S(2)}, u32[]{:S(2)}) collective-permute-start(bf16[4,128,256]{2,1,0:T(8,128)(2,1)S(1)} %get-tuple-element.34), channel_id=1, source_target_pairs={{0,3},{1,2},{2,1},{3,0},{4,7},{5,6},{6,5},{7,4},{8,11},{9,10},{10,... | collective-permute-start | bytes 786440 | tf_op jit(solution)/shard_map/ppermute | solution.py:273
  27.3 46.0 %collective-permute-start = (bf16[4,128,256]{2,1,0:T(8,128)(2,1)S(1)}, bf16[4,128,256]{2,1,0:T(8,128)(2,1)S(1)}, u32[]{:S(2)}, u32[]{:S(2)}) collective-permute-start(bf16[4,128,256]{2,1,0:T(8,128)(2,1)S(1)} %get-tuple-element.23), channel_id=1, source_target_pairs={{0,1},{1,0},{2,3},{3,2},{4,5},{5,4},{6,7},{7,6},{8,9},{9,8},{10,11... | collective-permute-start | bytes 786440 | tf_op jit(solution)/shard_map/ppermute | solution.py:273
  27.3 46.4 %collective-permute-start.1 = (bf16[4,128,256]{2,1,0:T(8,128)(2,1)S(1)}, bf16[4,128,256]{2,1,0:T(8,128)(2,1)S(1)}, u32[]{:S(2)}, u32[]{:S(2)}) collective-permute-start(bf16[4,128,256]{2,1,0:T(8,128)(2,1)S(1)} %get-tuple-element.24), channel_id=1, source_target_pairs={{0,2},{1,3},{2,0},{3,1},{4,6},{5,7},{6,4},{7,5},{8,10},{9,11},{10,... | collective-permute-start | bytes 786440 | tf_op jit(solution)/shard_map/ppermute | solution.py:273
  34.1 39.6 %collective-permute-start.2 = (bf16[4,128,256]{2,1,0:T(8,128)(2,1)S(1)}, bf16[4,128,256]{2,1,0:T(8,128)(2,1)S(1)}, u32[]{:S(2)}, u32[]{:S(2)}) collective-permute-start(bf16[4,128,256]{2,1,0:T(8,128)(2,1)S(1)} %get-tuple-element.25), channel_id=1, source_target_pairs={{0,3},{1,2},{2,1},{3,0},{4,7},{5,6},{6,5},{7,4},{8,11},{9,10},{10,... | collective-permute-start | bytes 786440 | tf_op jit(solution)/shard_map/ppermute | solution.py:273
  52.3 35.0 %collective-permute-start.12 = (bf16[2,128,256]{2,1,0:T(8,128)(2,1)S(1)}, bf16[2,128,256]{2,1,0:T(8,128)(2,1)S(1)}, u32[]{:S(2)}, u32[]{:S(2)}) collective-permute-start(bf16[2,128,256]{2,1,0:T(8,128)(2,1)S(1)} %get-tuple-element.36), channel_id=1, source_target_pairs={{0,3},{1,2},{2,1},{3,0},{4,7},{5,6},{6,5},{7,4},{8,11},{9,10},{10,... | collective-permute-start | bytes 393224 | tf_op jit(solution)/shard_map/ppermute | solution.py:273
  55.5 32.7 %collective-permute-start.13 = (bf16[2,128,256]{2,1,0:T(8,128)(2,1)S(1)}, bf16[2,128,256]{2,1,0:T(8,128)(2,1)S(1)}, u32[]{:S(2)}, u32[]{:S(2)}) collective-permute-start(bf16[2,128,256]{2,1,0:T(8,128)(2,1)S(1)} %get-tuple-element.37), channel_id=1, source_target_pairs={{0,2},{1,3},{2,0},{3,1},{4,6},{5,7},{6,4},{7,5},{8,10},{9,11},{10,... | collective-permute-start | bytes 393224 | tf_op jit(solution)/shard_map/ppermute | solution.py:273
  73.3 15.0 %collective-permute-start.14 = (bf16[2,128,256]{2,1,0:T(8,128)(2,1)S(1)}, bf16[2,128,256]{2,1,0:T(8,128)(2,1)S(1)}, u32[]{:S(2)}, u32[]{:S(2)}) collective-permute-start(bf16[2,128,256]{2,1,0:T(8,128)(2,1)S(1)} %get-tuple-element.38), channel_id=1, source_target_pairs={{0,1},{1,0},{2,3},{3,2},{4,5},{5,4},{6,7},{7,6},{8,9},{9,8},{10,11... | collective-permute-start | bytes 393224 | tf_op jit(solution)/shard_map/ppermute | solution.py:273
  78.4 10.8 %collective-permute-start.6 = (bf16[2,128,256]{2,1,0:T(8,128)(2,1)S(1)}, bf16[2,128,256]{2,1,0:T(8,128)(2,1)S(1)}, u32[]{:S(2)}, u32[]{:S(2)}) collective-permute-start(bf16[2,128,256]{2,1,0:T(8,128)(2,1)S(1)} %get-tuple-element.28), channel_id=1, source_target_pairs={{0,3},{1,2},{2,1},{3,0},{4,7},{5,6},{6,5},{7,4},{8,11},{9,10},{10,... | collective-permute-start | bytes 393224 | tf_op jit(solution)/shard_map/ppermute | solution.py:273
  80.9 15.7 %collective-permute-start.7 = (bf16[2,128,256]{2,1,0:T(8,128)(2,1)S(1)}, bf16[2,128,256]{2,1,0:T(8,128)(2,1)S(1)}, u32[]{:S(2)}, u32[]{:S(2)}) collective-permute-start(bf16[2,128,256]{2,1,0:T(8,128)(2,1)S(1)} %get-tuple-element.29), channel_id=1, source_target_pairs={{0,2},{1,3},{2,0},{3,1},{4,6},{5,7},{6,4},{7,5},{8,10},{9,11},{10,... | collective-permute-start | bytes 393224 | tf_op jit(solution)/shard_map/ppermute | solution.py:273
  87.4 9.2 %collective-permute-start.8 = (bf16[2,128,256]{2,1,0:T(8,128)(2,1)S(1)}, bf16[2,128,256]{2,1,0:T(8,128)(2,1)S(1)}, u32[]{:S(2)}, u32[]{:S(2)}) collective-permute-start(bf16[2,128,256]{2,1,0:T(8,128)(2,1)S(1)} %get-tuple-element.30), channel_id=1, source_target_pairs={{0,1},{1,0},{2,3},{3,2},{4,5},{5,4},{6,7},{7,6},{8,9},{9,8},{10,11... | collective-permute-start | bytes 393224 | tf_op jit(solution)/shard_map/ppermute | solution.py:273
where the time goes:
time: 97.5 us; the launch traced here: 97.3 us
  starting transfers between devices  51 us (52%)
  waiting for transfers between devices  27.8 us (29%)
  Pallas kernels  16.7 us (17%)
  between operations  1.47 us (2%)
    ppermute x15, starting transfers between devices, swap(): return lax.ppermute(array, 'seq', [(i, i ^ x) for i in range(n)])  51 us
    ppermute x15, waiting for transfers between devices, swap(): return lax.ppermute(array, 'seq', [(i, i ^ x) for i in range(n)])  27.8 us
    pallas_call x2, Pallas kernels, attend(): pl.pallas_call(functools.partial(attend_kernel, n=n), out_shape=tuple((ja...  9.38 us
    pallas_call x2, Pallas kernels, pack_values(): pl.pallas_call(kernel, out_shape=tuple((jax.ShapeDtypeStruct((len(arrays)...  2.91 us
    pallas_call x1, Pallas kernels, rope_packs(): pl.pallas_call(functools.partial(rope_kernel, n=n, sizes=sizes), out_shap...  2.69 us
  transfers between devices with their start and end apart: 15, of which 6 were waited for; matrix products, arithmetic and copies ran while one was open for 0% of the time, Pallas kernels for 15%

commit v1 on v0

--- a/solution.py
+++ b/solution.py
@@ -18,7 +18,8 @@
 rope_theta = 10000.0
 
 SIZES = (2, 2)
-ORDERS = {'v': (2, 3, 1), 'qk': (1, 2, 3), 'out': (3, 2, 1)}
+ORDERS = {"v": (3, 2, 1), "qk": (2, 3, 1), "out": (3, 2, 1)}
+LAST = ((3, (0, 3)), (2, None), (1, None), (3, (1, 2)))
 
 
 def rope_tables(first, count):
@@ -151,22 +152,23 @@
     vals = jnp.concatenate([v_ref[0]] + rows[0::2], axis=0)
     vdots = jnp.concatenate([vd_ref[0]] + rows[1::2], axis=0)
     vboth = jnp.concatenate([vals, vdots], axis=1)
+    q = jnp.concatenate([p[0] for p in packs], axis=0)
+    qd = jnp.concatenate([p[2] for p in packs], axis=0)
+    raw = dot_t(q, keys)
+    largest = jnp.max(raw, axis=-1, keepdims=True)
+    expons = jnp.exp2((raw - largest) * (scaling * math.log2(math.e)))
+    inverse = 1.0 / jnp.sum(expons, axis=-1, keepdims=True)
+    weights = (expons * inverse).astype(jnp.bfloat16)
+    scores_dot = dot_t(jnp.concatenate([qd, q], axis=1), both) * scaling
+    product = weights.astype(jnp.float32) * scores_dot
+    correction = jnp.sum(product, axis=-1, keepdims=True)
+    mixed = dot(weights, vboth)
+    out = mixed[:, :HD]
+    tangent = mixed[:, HD:] + dot(product.astype(jnp.bfloat16), vals) - correction * out
+    rows = out.shape[0] // n
     for x in range(n):
-        q = packs[x][0]
-        qd = packs[x][2]
-        raw = dot_t(q, keys)
-        largest = jnp.max(raw, axis=-1, keepdims=True)
-        expons = jnp.exp((raw - largest) * scaling)
-        inverse = 1.0 / jnp.sum(expons, axis=-1, keepdims=True)
-        weights = (expons * inverse).astype(jnp.bfloat16)
-        scores_dot = dot_t(jnp.concatenate([qd, q], axis=1), both) * scaling
-        product = weights.astype(jnp.float32) * scores_dot
-        correction = jnp.sum(product, axis=-1, keepdims=True)
-        mixed = dot(weights, vboth)
-        out = mixed[:, :HD]
-        tangent = mixed[:, HD:] + dot(product.astype(jnp.bfloat16), vals) - correction * out
-        outs[x][0] = out.astype(jnp.bfloat16)
-        outs[x][1] = tangent.astype(jnp.bfloat16)
+        outs[x][0] = out[x * rows : (x + 1) * rows].astype(jnp.bfloat16)
+        outs[x][1] = tangent[x * rows : (x + 1) * rows].astype(jnp.bfloat16)
 
 
 def attend(blocks, value, vdot, packs, values, start, heads, n):
@@ -206,26 +208,28 @@
 
 def place(pieces, width, tokens, into=None):
     shape = jax.ShapeDtypeStruct((1, tokens, H * HD), jnp.bfloat16)
-    total = sum(piece.shape[2] for _, _, piece in pieces)
+    total = sum(piece[2].shape[2] for piece in pieces)
 
     def kernel(*refs):
         ins, outs, sems = refs[: len(pieces)], refs[-3:-1], refs[-1]
         me = lax.axis_index("seq")
-        copies = []
-        for ref, (x, column, _) in zip(ins, pieces):
-            first = pl.multiple_of(jnp.bitwise_xor(me, x) * width + column, HD)
-            for a in range(2):
-                copies.append(
-                    pltpu.make_async_copy(
-                        ref.at[a],
-                        outs[a].at[0, :, pl.ds(first, ref.shape[2])],
-                        sems.at[len(copies)],
-                    )
-                )
-        for copy in copies:
-            copy.start()
-        for copy in copies:
-            copy.wait()
+        for act in ("start", "wait"):
+            for i, (ref, (x, column, _, members)) in enumerate(zip(ins, pieces)):
+
+                def copies(i=i, ref=ref, x=x, column=column):
+                    first = pl.multiple_of(jnp.bitwise_xor(me, x) * width + column, HD)
+                    for a in range(2):
+                        copy = pltpu.make_async_copy(
+                            ref.at[a],
+                            outs[a].at[0, :, pl.ds(first, ref.shape[2])],
+                            sems.at[2 * i + a],
+                        )
+                        getattr(copy, act)()
+
+                if members is None:
+                    copies()
+                else:
+                    pl.when(functools.reduce(jnp.logical_or, [me == m for m in members]))(copies)
 
     into = () if into is None else tuple(into)
     return pl.pallas_call(
@@ -241,12 +245,18 @@
             flops=0, bytes_accessed=8 * tokens * total, transcendentals=0
         ),
         name="place",
-    )(*(piece for _, _, piece in pieces), *into)
+    )(*(piece[2] for piece in pieces), *into)
 
 
 def chunk_sizes(n):
     per_device = H // n
     return SIZES if per_device == 4 else (1,) * per_device
+
+
+def routes(n, chunk):
+    if n == 4 and chunk == len(chunk_sizes(n)) - 1:
+        return LAST
+    return [(x, None) for x in partner_order(n, "out")]
 
 
 def partner_order(n, kind):
@@ -269,16 +279,19 @@
     value_hbm = pltpu.with_memory_space_constraint(value_states, pltpu.HBM)
     vdot_hbm = pltpu.with_memory_space_constraint(value_tangent, pltpu.HBM)
 
-    def swap(array, x):
-        return lax.ppermute(array, "seq", [(i, i ^ x) for i in range(n)])
-
-    value_in = {}
-    for xs in (order[:1], order[1:]):
-        wanted = [(x, (0, 1)) for x in xs]
-        if wanted:
-            sent = pack_values(value_hbm, vdot_hbm, wanted, tokens, width)
-            for x, array in zip(xs, sent):
-                value_in[x] = (swap(array, x),)
+    def swap(array, x, members=None):
+        pairs = [(i ^ x, i) for i in range(n) if members is None or i in members]
+        return lax.ppermute(array, "seq", pairs)
+
+    first, rest = order[0], order[1:]
+    column = jnp.bitwise_xor(me, first) * width
+    sliced = lax.dynamic_slice(value_states, (0, 0, column), (1, tokens, width))
+    value_in = {first: [swap(sliced, first)]}
+    wanted = [(first, (1,))] + [(x, (0, 1)) for x in rest]
+    sent = pack_values(value_hbm, vdot_hbm, wanted, tokens, width)
+    value_in[first].append(swap(sent[0], first))
+    for x, array in zip(rest, sent[1:]):
+        value_in[x] = [swap(array, x)]
 
     blocks = jnp.bitwise_xor(jnp.arange(n, dtype=jnp.int32), me.astype(jnp.int32))
     cosine, sine = rope_tables(offsets[0] + me * tokens, tokens)
@@ -302,9 +315,11 @@
             heads,
             n,
         )
-        early.append((0, start * HD, outs[0]))
+        early.append((0, start * HD, outs[0], None))
         last = early if c < len(sizes) - 1 else late
-        last += [(x, start * HD, swap(outs[x], x)) for x in partner_order(n, "out")]
+        for x, members in routes(n, c):
+            got = swap(outs[x], x, members)
+            last.append((x, start * HD, got, members))
     placed = place(early, width, tokens)
     return place(late, width, tokens, placed)
 

time: 97.5 us -> 102 us (1.046)
  local copies, waits for them, and re-layouts: 0.03 us -> 6.54 us
  waiting for transfers between devices: 27.8 us -> 33 us
  Pallas kernels: 16.7 us -> 12.8 us
  starting transfers between devices: 51 us -> 47.1 us
    unnamed x12 -> x26, local copies, waits for them, and re-layouts: 0.03 us -> 6.53 us
    ppermute x15 -> x17, waiting for transfers between devices: 27.8 us -> 33 us  [swap(): return lax.ppermute(array, 'seq', pairs)]
    ppermute x15 -> x17, starting transfers between devices: 51 us -> 47.1 us  [swap(): return lax.ppermute(array, 'seq', pairs)]
    pallas_call x2, Pallas kernels: 9.38 us -> 5.69 us  [attend(): pl.pallas_call(functools.partial(attend_kernel, n=n), out_shape=tuple((ja...]
    pallas_call x2 -> x1, Pallas kernels: 2.91 us -> 1.99 us  [pack_values(): pl.pallas_call(kernel, out_shape=tuple((jax.ShapeDtypeStruct((len(arrays)...]
  transfers between devices with their start and end apart: 15 -> 17, of which waited for: 6 -> 8; matrix products, arithmetic and copies ran while one was open for 0% -> 0% of each run, Pallas kernels for 15% -> 10%
where the time goes in v1:
time: 102 us; the launch traced here: 101 us
  starting transfers between devices  47.1 us (46%)
  waiting for transfers between devices  33 us (32%)
  Pallas kernels  12.8 us (13%)
  local copies, waits for them, and re-layouts  6.54 us (6%)
  between operations  1.44 us (1%)
    ppermute x17, starting transfers between devices, swap(): return lax.ppermute(array, 'seq', pairs)  47.1 us
    ppermute x17, waiting for transfers between devices, swap(): return lax.ppermute(array, 'seq', pairs)  33 us
    unnamed x26, local copies, waits for them, and re-layouts  6.53 us
    pallas_call x2, Pallas kernels, attend(): pl.pallas_call(functools.partial(attend_kernel, n=n), out_shape=tuple((ja...  5.69 us
    pallas_call x1, Pallas kernels, rope_packs(): pl.pallas_call(functools.partial(rope_kernel, n=n, sizes=sizes), out_shap...  3.36 us
  transfers between devices with their start and end apart: 17, of which 8 were waited for; matrix products, arithmetic and copies ran while one was open for 0% of the time, Pallas kernels for 10%

profile of v1, /device:TPU:0, one launch (start us, length us, event | category | flops | bytes accessed | tf_op | source)
XLA Modules:
  0.0 101.2 jit_solution(4769681220371504004)
XLA Ops:
  0.6 0.0 copy-start.2
  0.6 0.0 copy-start.1
  0.6 2.0 %pack_values.1 = (bf16[1,128,512]{2,1,0:T(8,128)(2,1)S(1)}, bf16[2,128,512]{2,1,0:T(8,128)(2,1)S(1)}, bf16[2,128,512]{2,1,0:T(8,128)(2,1)}) custom-call(bf16[1,128,2048]{2,1,0:T(8,128)(2,1)} %v_ref.5, bf16[1,128,2048]{2,1,0:T(8,128)(2,1)} %vd_ref.3), custom_call_target="tpu_custom_call" | custom-call | bytes 1310720 | tf_op jit(solution)/shard_map/pack_values/pallas_call | solution.py:70
  2.6 3.1 %collective-permute-start.3 = (bf16[2,128,512]{2,1,0:T(8,128)(2,1)}, bf16[2,128,512]{2,1,0:T(8,128)(2,1)S(1)}, u32[]{:S(2)}, u32[]{:S(2)}) collective-permute-start(bf16[2,128,512]{2,1,0:T(8,128)(2,1)} %get-tuple-element.27), channel_id=1, source_target_pairs={{1,0},{0,1},{3,2},{2,3},{5,4},{4,5},{7,6},{6,7},{9,8},{8,9},{11,10... | collective-permute-start | bytes 786440 | tf_op jit(solution)/shard_map/ppermute | solution.py:284
  5.8 2.6 %collective-permute-start.4 = (bf16[2,128,512]{2,1,0:T(8,128)(2,1)S(1)}, bf16[2,128,512]{2,1,0:T(8,128)(2,1)S(1)}, u32[]{:S(2)}, u32[]{:S(2)}) collective-permute-start(bf16[2,128,512]{2,1,0:T(8,128)(2,1)S(1)} %get-tuple-element.28), channel_id=1, source_target_pairs={{2,0},{3,1},{0,2},{1,3},{6,4},{7,5},{4,6},{5,7},{10,8},{11,9},{8,1... | collective-permute-start | bytes 786440 | tf_op jit(solution)/shard_map/ppermute | solution.py:284
  9.1 0.3 fusion
  9.4 0.0 copy-done.2
  9.5 0.0 copy-done.1
  9.5 0.0 copy-start.3
  9.5 1.0 %copy-done.3 = bf16[1,128,2048]{2,1,0:T(8,128)(2,1)S(1)} copy-done((bf16[1,128,2048]{2,1,0:T(8,128)(2,1)S(1)}, bf16[1,128,2048]{2,1,0:T(8,128)(2,1)}, u32[]{:S(2)}) %copy-start.3) | copy-done | bytes 524312
  10.5 1.0 %copy-done.4 = bf16[1,128,2048]{2,1,0:T(8,128)(2,1)S(1)} copy-done((bf16[1,128,2048]{2,1,0:T(8,128)(2,1)S(1)}, bf16[1,128,2048]{2,1,0:T(8,128)(2,1)}, u32[]{:S(2)}) %copy-start.4) | copy-done | bytes 524312
  11.6 0.0 copy-start
  11.6 0.0 copy-start.5
  11.6 3.4 %rope_packs.1 = (bf16[4,128,256]{2,1,0:T(8,128)(2,1)S(1)}, bf16[4,128,256]{2,1,0:T(8,128)(2,1)}, bf16[4,128,256]{2,1,0:T(8,128)(2,1)S(1)}, bf16[4,128,256]{2,1,0...) custom-call(s32[4]{0:T(128)S(1)} %iota_xor_fusion.blk_ref, ...), custom_call_target="tpu_custom_call" | custom-call | flops 6291456 | bytes 4194304 | tf_op jit(solution)/shard_map/rope_packs/pallas_call | solution.py:116
  14.9 0.0 copy-start.6
  14.9 0.7 copy-done.6
  15.6 0.0 copy-start.8
  15.6 0.7 copy-done.8
  16.3 0.0 copy-start.9
  16.3 0.7 copy-done.9
  17.0 0.0 copy-start.11
  17.0 0.7 copy-done.11
  17.7 0.0 copy-start.12
  17.7 0.7 copy-done.12
  18.4 0.4 collective-permute-start.11
  18.9 0.0 copy-done
  18.9 1.4 %collective-permute-start.5 = (bf16[1,128,512]{2,1,0:T(8,128)(2,1)S(1)}, bf16[1,128,512]{2,1,0:T(8,128)(2,1)S(1)}, u32[]{:S(2)}, u32[]{:S(2)}) collective-permute-start(bf16[1,128,512]{2,1,0:T(8,128)(2,1)S(1)} %constant_dynamic-slice_fusion), channel_id=1, source_target_pairs={{3,0},{2,1},{1,2},{0,3},{7,4},{6,5},{5,6},{4,7},{11,8},{10,9},{9,1... | collective-permute-start | bytes 393224 | tf_op jit(solution)/shard_map/ppermute | solution.py:284
  20.3 2.5 %collective-permute-start.6 = (bf16[1,128,512]{2,1,0:T(8,128)(2,1)S(1)}, bf16[1,128,512]{2,1,0:T(8,128)(2,1)S(1)}, u32[]{:S(2)}, u32[]{:S(2)}) collective-permute-start(bf16[1,128,512]{2,1,0:T(8,128)(2,1)S(1)} %get-tuple-element.29), channel_id=1, source_target_pairs={{3,0},{2,1},{1,2},{0,3},{7,4},{6,5},{5,6},{4,7},{11,8},{10,9},{9,1... | collective-permute-start | bytes 393224 | tf_op jit(solution)/shard_map/ppermute | solution.py:284
  22.8 7.4 %collective-permute-done.5.refs_6_ = bf16[1,128,512]{2,1,0:T(8,128)(2,1)S(1)} collective-permute-done((bf16[1,128,512]{2,1,0:T(8,128)(2,1)S(1)}, bf16[1,128,512]{2,1,0:T(8,128)(2,1)S(1)}, u32[]{:S(2)}, u32[]{:S(2)}) %collective-permute-start.5) | collective-permute-done | bytes 131104 | tf_op jit(solution)/shard_map/ppermute | solution.py:284
  30.2 0.0 collective-permute-start.12
  30.2 2.6 %collective-permute-done.6.refs_7_ = bf16[1,128,512]{2,1,0:T(8,128)(2,1)S(1)} collective-permute-done((bf16[1,128,512]{2,1,0:T(8,128)(2,1)S(1)}, bf16[1,128,512]{2,1,0:T(8,128)(2,1)S(1)}, u32[]{:S(2)}, u32[]{:S(2)}) %collective-permute-start.6) | collective-permute-done | bytes 131104 | tf_op jit(solution)/shard_map/ppermute | solution.py:284
  32.8 3.0 %collective-permute-start.13 = (bf16[4,128,256]{2,1,0:T(8,128)(2,1)}, bf16[4,128,256]{2,1,0:T(8,128)(2,1)S(1)}, u32[]{:S(2)}, u32[]{:S(2)}) collective-permute-start(bf16[4,128,256]{2,1,0:T(8,128)(2,1)} %copy-done.11), channel_id=1, source_target_pairs={{3,0},{2,1},{1,2},{0,3},{7,4},{6,5},{5,6},{4,7},{11,8},{10,9},{9,1... | collective-permute-start | bytes 786440 | tf_op jit(solution)/shard_map/ppermute | solution.py:284
  35.8 0.0 collective-permute-done.3.refs_4_
  35.8 9.3 %collective-permute-start = (bf16[4,128,256]{2,1,0:T(8,128)(2,1)}, bf16[4,128,256]{2,1,0:T(8,128)(2,1)S(1)}, u32[]{:S(2)}, u32[]{:S(2)}) collective-permute-start(bf16[4,128,256]{2,1,0:T(8,128)(2,1)} %copy-done.8), channel_id=1, source_target_pairs={{1,0},{0,1},{3,2},{2,3},{5,4},{4,5},{7,6},{6,7},{9,8},{8,9},{11,10... | collective-permute-start | bytes 786440 | tf_op jit(solution)/shard_map/ppermute | solution.py:284
  45.1 0.0 collective-permute-done.4.refs_5_
  45.1 0.0 copy-done.7
  45.1 1.5 %collective-permute-start.1 = (bf16[4,128,256]{2,1,0:T(8,128)(2,1)S(1)}, bf16[4,128,256]{2,1,0:T(8,128)(2,1)S(1)}, u32[]{:S(2)}, u32[]{:S(2)}) collective-permute-start(bf16[4,128,256]{2,1,0:T(8,128)(2,1)S(1)} %copy-done.7), channel_id=1, source_target_pairs={{2,0},{3,1},{0,2},{1,3},{6,4},{7,5},{4,6},{5,7},{10,8},{11,9},{8,1... | collective-permute-start | bytes 786440 | tf_op jit(solution)/shard_map/ppermute | solution.py:284
  46.6 0.0 collective-permute-done.11.refs_1_
  46.6 1.5 %collective-permute-start.2 = (bf16[4,128,256]{2,1,0:T(8,128)(2,1)S(1)}, bf16[4,128,256]{2,1,0:T(8,128)(2,1)S(1)}, u32[]{:S(2)}, u32[]{:S(2)}) collective-permute-start(bf16[4,128,256]{2,1,0:T(8,128)(2,1)S(1)} %get-tuple-element.26), channel_id=1, source_target_pairs={{3,0},{2,1},{1,2},{0,3},{7,4},{6,5},{5,6},{4,7},{11,8},{10,9},{9,1... | collective-permute-start | bytes 786440 | tf_op jit(solution)/shard_map/ppermute | solution.py:284
  48.1 14.0 %collective-permute-done.12.refs_2_ = bf16[4,128,256]{2,1,0:T(8,128)(2,1)S(1)} collective-permute-done((bf16[4,128,256]{2,1,0:T(8,128)(2,1)}, bf16[4,128,256]{2,1,0:T(8,128)(2,1)S(1)}, u32[]{:S(2)}, u32[]{:S(2)}) %collective-permute-start.12) | collective-permute-done | bytes 262176 | tf_op jit(solution)/shard_map/ppermute | solution.py:284
  62.1 0.0 collective-permute-done.13.refs_3_
  62.1 0.0 copy-done.5
  62.1 0.9 copy-done.10
  63.1 2.8 %attend.3 = (bf16[2,128,256]{2,1,0:T(8,128)(2,1)S(1)}, bf16[2,128,256]{2,1,0:T(8,128)(2,1)S(1)}, bf16[2,128,256]{2,1,0:T(8,128)(2,1)S(1)}, bf16[2,128,256]{2,1,0:T(8,128)(2,1)S(1)}) custom-call(s32[4]{0:T(128)S(1)} %iota_xor_fusion.blk_ref, bf16[1,128,2048]{2,1,0:T(8,128)(2,1)S(1)} %copy-done, bf16[1,128,2048]{2,1,0:T(8,128)(2,1)S(1)} %copy-done.5, ...), custom_call_target="tpu_custom_call" | custom-call | flops 805306368 | bytes 2097152 | tf_op jit(solution)/shard_map/attend/pallas_call | solution.py:188
  65.9 0.2 collective-permute-start.14
  66.1 8.9 %collective-permute-start.15 = (bf16[2,128,256]{2,1,0:T(8,128)(2,1)S(1)}, bf16[2,128,256]{2,1,0:T(8,128)(2,1)S(1)}, u32[]{:S(2)}, u32[]{:S(2)}) collective-permute-start(bf16[2,128,256]{2,1,0:T(8,128)(2,1)S(1)} %get-tuple-element.39), channel_id=1, source_target_pairs={{2,0},{3,1},{0,2},{1,3},{6,4},{7,5},{4,6},{5,7},{10,8},{11,9},{8,1... | collective-permute-start | bytes 393224 | tf_op jit(solution)/shard_map/ppermute | solution.py:284
  75.0 0.0 collective-permute-done.refs_1_
  75.0 2.6 %collective-permute-done.1.refs_2_ = bf16[4,128,256]{2,1,0:T(8,128)(2,1)S(1)} collective-permute-done((bf16[4,128,256]{2,1,0:T(8,128)(2,1)S(1)}, bf16[4,128,256]{2,1,0:T(8,128)(2,1)S(1)}, u32[]{:S(2)}, u32[]{:S(2)}) %collective-permute-start.1) | collective-permute-done | bytes 262176 | tf_op jit(solution)/shard_map/ppermute | solution.py:284
  77.6 0.0 collective-permute-done.2.refs_3_
  77.6 2.9 %attend.2 = (bf16[2,128,256]{2,1,0:T(8,128)(2,1)S(1)}, bf16[2,128,256]{2,1,0:T(8,128)(2,1)S(1)}, bf16[2,128,256]{2,1,0:T(8,128)(2,1)S(1)}, bf16[2,128,256]{2,1,0:T(8,128)(2,1)S(1)}) custom-call(s32[4]{0:T(128)S(1)} %iota_xor_fusion.blk_ref, bf16[1,128,2048]{2,1,0:T(8,128)(2,1)S(1)} %copy-done, bf16[1,128,2048]{2,1,0:T(8,128)(2,1)S(1)} %copy-done.5, ...), custom_call_target="tpu_custom_call" | custom-call | flops 805306368 | bytes 2097152 | tf_op jit(solution)/shard_map/attend/pallas_call | solution.py:188
  80.4 6.6 %collective-permute-start.8 = (bf16[2,128,256]{2,1,0:T(8,128)(2,1)S(1)}, bf16[2,128,256]{2,1,0:T(8,128)(2,1)S(1)}, u32[]{:S(2)}, u32[]{:S(2)}) collective-permute-start(bf16[2,128,256]{2,1,0:T(8,128)(2,1)S(1)} %get-tuple-element.31), channel_id=1, source_target_pairs={{2,0},{3,1},{0,2},{1,3},{6,4},{7,5},{4,6},{5,7},{10,8},{11,9},{8,1... | collective-permute-start | bytes 393224 | tf_op jit(solution)/shard_map/ppermute | solution.py:284
  87.1 1.1 %collective-permute-start.16 = (bf16[2,128,256]{2,1,0:T(8,128)(2,1)S(1)}, bf16[2,128,256]{2,1,0:T(8,128)(2,1)S(1)}, u32[]{:S(2)}, u32[]{:S(2)}) collective-permute-start(bf16[2,128,256]{2,1,0:T(8,128)(2,1)S(1)} %get-tuple-element.40), channel_id=1, source_target_pairs={{1,0},{0,1},{3,2},{2,3},{5,4},{4,5},{7,6},{6,7},{9,8},{8,9},{11,10... | collective-permute-start | bytes 393224 | tf_op jit(solution)/shard_map/ppermute | solution.py:284
  88.2 0.9 collective-permute-start.9
  89.1 0.0 collective-permute-done.14.refs_1_
  89.1 0.7 collective-permute-start.10
  89.7 1.9 %collective-permute-done.15.refs_2_ = bf16[2,128,256]{2,1,0:T(8,128)(2,1)S(1)} collective-permute-done((bf16[2,128,256]{2,1,0:T(8,128)(2,1)S(1)}, bf16[2,128,256]{2,1,0:T(8,128)(2,1)S(1)}, u32[]{:S(2)}, u32[]{:S(2)}) %collective-permute-start.15) | collective-permute-done | bytes 131104 | tf_op jit(solution)/shard_map/ppermute | solution.py:284
  91.7 3.4 %collective-permute-start.7 = (bf16[2,128,256]{2,1,0:T(8,128)(2,1)S(1)}, bf16[2,128,256]{2,1,0:T(8,128)(2,1)S(1)}, u32[]{:S(2)}, u32[]{:S(2)}) collective-permute-start(bf16[2,128,256]{2,1,0:T(8,128)(2,1)S(1)} %get-tuple-element.30), channel_id=1, source_target_pairs={{3,0},{0,3},{7,4},{4,7},{11,8},{8,11},{15,12},{12,15},{19,16},{16,... | collective-permute-start | bytes 393224 | tf_op jit(solution)/shard_map/ppermute | solution.py:284
  95.1 2.3 %collective-permute-done.16.refs_3_ = bf16[2,128,256]{2,1,0:T(8,128)(2,1)S(1)} collective-permute-done((bf16[2,128,256]{2,1,0:T(8,128)(2,1)S(1)}, bf16[2,128,256]{2,1,0:T(8,128)(2,1)S(1)}, u32[]{:S(2)}, u32[]{:S(2)}) %collective-permute-start.16) | collective-permute-done | bytes 131104 | tf_op jit(solution)/shard_map/ppermute | solution.py:284
  97.3 0.9 place.2
  98.3 0.0 collective-permute-done.8.refs_1_
  98.3 0.8 collective-permute-done.9.refs_2_
  99.0 0.0 collective-permute-done.10.refs_3_
  99.0 1.4 %collective-permute-done.7.refs_0_ = bf16[2,128,256]{2,1,0:T(8,128)(2,1)S(1)} collective-permute-done((bf16[2,128,256]{2,1,0:T(8,128)(2,1)S(1)}, bf16[2,128,256]{2,1,0:T(8,128)(2,1)S(1)}, u32[]{:S(2)}, u32[]{:S(2)}) %collective-permute-start.7) | collective-permute-done | bytes 131104 | tf_op jit(solution)/shard_map/ppermute | solution.py:284
  100.4 0.8 place.3
  (9 shorter events, 0.1 us)
Async XLA Ops:
  0.6 8.8 %copy-start.2 = (bf16[1,128,2048]{2,1,0:T(8,128)(2,1)S(1)}, bf16[1,128,2048]{2,1,0:T(8,128)(2,1)}, u32[]{:S(2)}) copy-start(bf16[1,128,2048]{2,1,0:T(8,128)(2,1)} %k_ref.1) | copy-start | bytes 1572868
  0.6 8.8 %copy-start.1 = (bf16[1,128,2048]{2,1,0:T(8,128)(2,1)S(1)}, bf16[1,128,2048]{2,1,0:T(8,128)(2,1)}, u32[]{:S(2)}) copy-start(bf16[1,128,2048]{2,1,0:T(8,128)(2,1)} %q_ref.1) | copy-start | bytes 1572868
  2.6 33.1 %collective-permute-start.3 = (bf16[2,128,512]{2,1,0:T(8,128)(2,1)}, bf16[2,128,512]{2,1,0:T(8,128)(2,1)S(1)}, u32[]{:S(2)}, u32[]{:S(2)}) collective-permute-start(bf16[2,128,512]{2,1,0:T(8,128)(2,1)} %get-tuple-element.27), channel_id=1, source_target_pairs={{1,0},{0,1},{3,2},{2,3},{5,4},{4,5},{7,6},{6,7},{9,8},{8,9},{11,10... | collective-permute-start | bytes 786440 | tf_op jit(solution)/shard_map/ppermute | solution.py:284
  5.8 39.3 %collective-permute-start.4 = (bf16[2,128,512]{2,1,0:T(8,128)(2,1)S(1)}, bf16[2,128,512]{2,1,0:T(8,128)(2,1)S(1)}, u32[]{:S(2)}, u32[]{:S(2)}) collective-permute-start(bf16[2,128,512]{2,1,0:T(8,128)(2,1)S(1)} %get-tuple-element.28), channel_id=1, source_target_pairs={{2,0},{3,1},{0,2},{1,3},{6,4},{7,5},{4,6},{5,7},{10,8},{11,9},{8,1... | collective-permute-start | bytes 786440 | tf_op jit(solution)/shard_map/ppermute | solution.py:284
  9.5 1.0 %copy-start.3 = (bf16[1,128,2048]{2,1,0:T(8,128)(2,1)S(1)}, bf16[1,128,2048]{2,1,0:T(8,128)(2,1)}, u32[]{:S(2)}) copy-start(bf16[1,128,2048]{2,1,0:T(8,128)(2,1)} %qd_ref.1) | copy-start | bytes 1572868
  10.5 1.0 %copy-start.4 = (bf16[1,128,2048]{2,1,0:T(8,128)(2,1)S(1)}, bf16[1,128,2048]{2,1,0:T(8,128)(2,1)}, u32[]{:S(2)}) copy-start(bf16[1,128,2048]{2,1,0:T(8,128)(2,1)} %kd_ref.1) | copy-start | bytes 1572868
  11.6 7.3 %copy-start = (bf16[1,128,2048]{2,1,0:T(8,128)(2,1)S(1)}, bf16[1,128,2048]{2,1,0:T(8,128)(2,1)}, u32[]{:S(2)}) copy-start(bf16[1,128,2048]{2,1,0:T(8,128)(2,1)} %v_ref.5) | copy-start | bytes 1572868
  11.6 50.5 %copy-start.5 = (bf16[1,128,2048]{2,1,0:T(8,128)(2,1)S(1)}, bf16[1,128,2048]{2,1,0:T(8,128)(2,1)}, u32[]{:S(2)}) copy-start(bf16[1,128,2048]{2,1,0:T(8,128)(2,1)} %vd_ref.3) | copy-start | bytes 1572868
  14.9 0.7 copy-start.6
  15.6 0.7 copy-start.8
  16.3 0.7 copy-start.9
  17.0 0.7 copy-start.11
  17.7 0.7 copy-start.12
  18.4 26.7 %copy-start.7 = (bf16[4,128,256]{2,1,0:T(8,128)(2,1)S(1)}, bf16[4,128,256]{2,1,0:T(8,128)(2,1)}, u32[]{:S(2)}) copy-start(bf16[4,128,256]{2,1,0:T(8,128)(2,1)} %copy-done.6) | copy-start | bytes 786436
  18.4 28.2 %collective-permute-start.11 = (bf16[4,128,256]{2,1,0:T(8,128)(2,1)}, bf16[4,128,256]{2,1,0:T(8,128)(2,1)S(1)}, u32[]{:S(2)}, u32[]{:S(2)}) collective-permute-start(bf16[4,128,256]{2,1,0:T(8,128)(2,1)} %get-tuple-element.34), channel_id=1, source_target_pairs={{1,0},{0,1},{3,2},{2,3},{5,4},{4,5},{7,6},{6,7},{9,8},{8,9},{11,10... | collective-permute-start | bytes 786440 | tf_op jit(solution)/shard_map/ppermute | solution.py:284
  18.9 11.3 %collective-permute-start.5 = (bf16[1,128,512]{2,1,0:T(8,128)(2,1)S(1)}, bf16[1,128,512]{2,1,0:T(8,128)(2,1)S(1)}, u32[]{:S(2)}, u32[]{:S(2)}) collective-permute-start(bf16[1,128,512]{2,1,0:T(8,128)(2,1)S(1)} %constant_dynamic-slice_fusion), channel_id=1, source_target_pairs={{3,0},{2,1},{1,2},{0,3},{7,4},{6,5},{5,6},{4,7},{11,8},{10,9},{9,1... | collective-permute-start | bytes 393224 | tf_op jit(solution)/shard_map/ppermute | solution.py:284
  20.3 12.5 %collective-permute-start.6 = (bf16[1,128,512]{2,1,0:T(8,128)(2,1)S(1)}, bf16[1,128,512]{2,1,0:T(8,128)(2,1)S(1)}, u32[]{:S(2)}, u32[]{:S(2)}) collective-permute-start(bf16[1,128,512]{2,1,0:T(8,128)(2,1)S(1)} %get-tuple-element.29), channel_id=1, source_target_pairs={{3,0},{2,1},{1,2},{0,3},{7,4},{6,5},{5,6},{4,7},{11,8},{10,9},{9,1... | collective-permute-start | bytes 393224 | tf_op jit(solution)/shard_map/ppermute | solution.py:284
  30.2 31.9 %collective-permute-start.12 = (bf16[4,128,256]{2,1,0:T(8,128)(2,1)}, bf16[4,128,256]{2,1,0:T(8,128)(2,1)S(1)}, u32[]{:S(2)}, u32[]{:S(2)}) collective-permute-start(bf16[4,128,256]{2,1,0:T(8,128)(2,1)} %copy-done.12), channel_id=1, source_target_pairs={{2,0},{3,1},{0,2},{1,3},{6,4},{7,5},{4,6},{5,7},{10,8},{11,9},{8,1... | collective-permute-start | bytes 786440 | tf_op jit(solution)/shard_map/ppermute | solution.py:284
  32.8 29.3 %collective-permute-start.13 = (bf16[4,128,256]{2,1,0:T(8,128)(2,1)}, bf16[4,128,256]{2,1,0:T(8,128)(2,1)S(1)}, u32[]{:S(2)}, u32[]{:S(2)}) collective-permute-start(bf16[4,128,256]{2,1,0:T(8,128)(2,1)} %copy-done.11), channel_id=1, source_target_pairs={{3,0},{2,1},{1,2},{0,3},{7,4},{6,5},{5,6},{4,7},{11,8},{10,9},{9,1... | collective-permute-start | bytes 786440 | tf_op jit(solution)/shard_map/ppermute | solution.py:284
  35.8 39.2 %collective-permute-start = (bf16[4,128,256]{2,1,0:T(8,128)(2,1)}, bf16[4,128,256]{2,1,0:T(8,128)(2,1)S(1)}, u32[]{:S(2)}, u32[]{:S(2)}) collective-permute-start(bf16[4,128,256]{2,1,0:T(8,128)(2,1)} %copy-done.8), channel_id=1, source_target_pairs={{1,0},{0,1},{3,2},{2,3},{5,4},{4,5},{7,6},{6,7},{9,8},{8,9},{11,10... | collective-permute-start | bytes 786440 | tf_op jit(solution)/shard_map/ppermute | solution.py:284
  45.1 32.5 %collective-permute-start.1 = (bf16[4,128,256]{2,1,0:T(8,128)(2,1)S(1)}, bf16[4,128,256]{2,1,0:T(8,128)(2,1)S(1)}, u32[]{:S(2)}, u32[]{:S(2)}) collective-permute-start(bf16[4,128,256]{2,1,0:T(8,128)(2,1)S(1)} %copy-done.7), channel_id=1, source_target_pairs={{2,0},{3,1},{0,2},{1,3},{6,4},{7,5},{4,6},{5,7},{10,8},{11,9},{8,1... | collective-permute-start | bytes 786440 | tf_op jit(solution)/shard_map/ppermute | solution.py:284
  46.6 30.9 %collective-permute-start.2 = (bf16[4,128,256]{2,1,0:T(8,128)(2,1)S(1)}, bf16[4,128,256]{2,1,0:T(8,128)(2,1)S(1)}, u32[]{:S(2)}, u32[]{:S(2)}) collective-permute-start(bf16[4,128,256]{2,1,0:T(8,128)(2,1)S(1)} %get-tuple-element.26), channel_id=1, source_target_pairs={{3,0},{2,1},{1,2},{0,3},{7,4},{6,5},{5,6},{4,7},{11,8},{10,9},{9,1... | collective-permute-start | bytes 786440 | tf_op jit(solution)/shard_map/ppermute | solution.py:284
  62.1 1.0 copy-start.10
  65.9 23.2 %collective-permute-start.14 = (bf16[2,128,256]{2,1,0:T(8,128)(2,1)S(1)}, bf16[2,128,256]{2,1,0:T(8,128)(2,1)S(1)}, u32[]{:S(2)}, u32[]{:S(2)}) collective-permute-start(bf16[2,128,256]{2,1,0:T(8,128)(2,1)S(1)} %get-tuple-element.38), channel_id=1, source_target_pairs={{3,0},{2,1},{1,2},{0,3},{7,4},{6,5},{5,6},{4,7},{11,8},{10,9},{9,1... | collective-permute-start | bytes 393224 | tf_op jit(solution)/shard_map/ppermute | solution.py:284
  66.1 25.6 %collective-permute-start.15 = (bf16[2,128,256]{2,1,0:T(8,128)(2,1)S(1)}, bf16[2,128,256]{2,1,0:T(8,128)(2,1)S(1)}, u32[]{:S(2)}, u32[]{:S(2)}) collective-permute-start(bf16[2,128,256]{2,1,0:T(8,128)(2,1)S(1)} %get-tuple-element.39), channel_id=1, source_target_pairs={{2,0},{3,1},{0,2},{1,3},{6,4},{7,5},{4,6},{5,7},{10,8},{11,9},{8,1... | collective-permute-start | bytes 393224 | tf_op jit(solution)/shard_map/ppermute | solution.py:284
  80.4 17.8 %collective-permute-start.8 = (bf16[2,128,256]{2,1,0:T(8,128)(2,1)S(1)}, bf16[2,128,256]{2,1,0:T(8,128)(2,1)S(1)}, u32[]{:S(2)}, u32[]{:S(2)}) collective-permute-start(bf16[2,128,256]{2,1,0:T(8,128)(2,1)S(1)} %get-tuple-element.31), channel_id=1, source_target_pairs={{2,0},{3,1},{0,2},{1,3},{6,4},{7,5},{4,6},{5,7},{10,8},{11,9},{8,1... | collective-permute-start | bytes 393224 | tf_op jit(solution)/shard_map/ppermute | solution.py:284
  87.1 10.3 %collective-permute-start.16 = (bf16[2,128,256]{2,1,0:T(8,128)(2,1)S(1)}, bf16[2,128,256]{2,1,0:T(8,128)(2,1)S(1)}, u32[]{:S(2)}, u32[]{:S(2)}) collective-permute-start(bf16[2,128,256]{2,1,0:T(8,128)(2,1)S(1)} %get-tuple-element.40), channel_id=1, source_target_pairs={{1,0},{0,1},{3,2},{2,3},{5,4},{4,5},{7,6},{6,7},{9,8},{8,9},{11,10... | collective-permute-start | bytes 393224 | tf_op jit(solution)/shard_map/ppermute | solution.py:284
  88.2 10.9 %collective-permute-start.9 = (bf16[2,128,256]{2,1,0:T(8,128)(2,1)S(1)}, bf16[2,128,256]{2,1,0:T(8,128)(2,1)S(1)}, u32[]{:S(2)}, u32[]{:S(2)}) collective-permute-start(bf16[2,128,256]{2,1,0:T(8,128)(2,1)S(1)} %get-tuple-element.32), channel_id=1, source_target_pairs={{1,0},{0,1},{3,2},{2,3},{5,4},{4,5},{7,6},{6,7},{9,8},{8,9},{11,10... | collective-permute-start | bytes 393224 | tf_op jit(solution)/shard_map/ppermute | solution.py:284
  89.1 10.0 %collective-permute-start.10 = (bf16[2,128,256]{2,1,0:T(8,128)(2,1)S(1)}, bf16[2,128,256]{2,1,0:T(8,128)(2,1)S(1)}, u32[]{:S(2)}, u32[]{:S(2)}) collective-permute-start(bf16[2,128,256]{2,1,0:T(8,128)(2,1)S(1)} %get-tuple-element.30), channel_id=1, source_target_pairs={{2,1},{1,2},{6,5},{5,6},{10,9},{9,10},{14,13},{13,14},{18,17},{17,... | collective-permute-start | bytes 393224 | tf_op jit(solution)/shard_map/ppermute | solution.py:284
  91.7 8.7 %collective-permute-start.7 = (bf16[2,128,256]{2,1,0:T(8,128)(2,1)S(1)}, bf16[2,128,256]{2,1,0:T(8,128)(2,1)S(1)}, u32[]{:S(2)}, u32[]{:S(2)}) collective-permute-start(bf16[2,128,256]{2,1,0:T(8,128)(2,1)S(1)} %get-tuple-element.30), channel_id=1, source_target_pairs={{3,0},{0,3},{7,4},{4,7},{11,8},{8,11},{15,12},{12,15},{19,16},{16,... | collective-permute-start | bytes 393224 | tf_op jit(solution)/shard_map/ppermute | solution.py:284

commit v2 on v1

--- a/solution.py
+++ b/solution.py
@@ -18,7 +18,7 @@
 rope_theta = 10000.0
 
 SIZES = (2, 2)
-ORDERS = {"v": (3, 2, 1), "qk": (2, 3, 1), "out": (3, 2, 1)}
+ORDERS = {"v": (3, 1, 2), "qk": (2, 3, 1), "out": (3, 2, 1)}
 LAST = ((3, (0, 3)), (2, None), (1, None), (3, (1, 2)))
 
 
@@ -152,23 +152,22 @@
     vals = jnp.concatenate([v_ref[0]] + rows[0::2], axis=0)
     vdots = jnp.concatenate([vd_ref[0]] + rows[1::2], axis=0)
     vboth = jnp.concatenate([vals, vdots], axis=1)
-    q = jnp.concatenate([p[0] for p in packs], axis=0)
-    qd = jnp.concatenate([p[2] for p in packs], axis=0)
-    raw = dot_t(q, keys)
-    largest = jnp.max(raw, axis=-1, keepdims=True)
-    expons = jnp.exp2((raw - largest) * (scaling * math.log2(math.e)))
-    inverse = 1.0 / jnp.sum(expons, axis=-1, keepdims=True)
-    weights = (expons * inverse).astype(jnp.bfloat16)
-    scores_dot = dot_t(jnp.concatenate([qd, q], axis=1), both) * scaling
-    product = weights.astype(jnp.float32) * scores_dot
-    correction = jnp.sum(product, axis=-1, keepdims=True)
-    mixed = dot(weights, vboth)
-    out = mixed[:, :HD]
-    tangent = mixed[:, HD:] + dot(product.astype(jnp.bfloat16), vals) - correction * out
-    rows = out.shape[0] // n
     for x in range(n):
-        outs[x][0] = out[x * rows : (x + 1) * rows].astype(jnp.bfloat16)
-        outs[x][1] = tangent[x * rows : (x + 1) * rows].astype(jnp.bfloat16)
+        q = packs[x][0]
+        qd = packs[x][2]
+        raw = dot_t(q, keys)
+        largest = jnp.max(raw, axis=-1, keepdims=True)
+        expons = jnp.exp((raw - largest) * scaling)
+        inverse = 1.0 / jnp.sum(expons, axis=-1, keepdims=True)
+        weights = (expons * inverse).astype(jnp.bfloat16)
+        scores_dot = dot_t(jnp.concatenate([qd, q], axis=1), both) * scaling
+        product = weights.astype(jnp.float32) * scores_dot
+        correction = jnp.sum(product, axis=-1, keepdims=True)
+        mixed = dot(weights, vboth)
+        out = mixed[:, :HD]
+        tangent = mixed[:, HD:] + dot(product.astype(jnp.bfloat16), vals) - correction * out
+        outs[x][0] = out.astype(jnp.bfloat16)
+        outs[x][1] = tangent.astype(jnp.bfloat16)
 
 
 def attend(blocks, value, vdot, packs, values, start, heads, n):

time: 102 us -> 103 us (level)
  waiting for transfers between devices: 33 us -> 28.1 us
  Pallas kernels: 12.8 us -> 16.5 us
  starting transfers between devices: 47.1 us -> 49.7 us
    ppermute x17, waiting for transfers between devices: 33 us -> 28.1 us  [swap(): return lax.ppermute(array, 'seq', pairs)]
    pallas_call x2, Pallas kernels: 5.69 us -> 9.41 us  [attend(): pl.pallas_call(functools.partial(attend_kernel, n=n), out_shape=tuple((ja...]
    ppermute x17, starting transfers between devices: 47.1 us -> 49.7 us  [swap(): return lax.ppermute(array, 'seq', pairs)]
  transfers between devices with their start and end apart: 17 -> 17, of which waited for: 8 -> 5; matrix products, arithmetic and copies ran while one was open for 0% -> 0% of each run, Pallas kernels for 10% -> 13%
where the time goes in v2:
time: 103 us
  starting transfers between devices  49.7 us (48%)
  waiting for transfers between devices  28.1 us (27%)
  Pallas kernels  16.5 us (16%)
  local copies, waits for them, and re-layouts  6.54 us (6%)
  between operations  1.46 us (1%)
    ppermute x17, starting transfers between devices, swap(): return lax.ppermute(array, 'seq', pairs)  49.7 us
    ppermute x17, waiting for transfers between devices, swap(): return lax.ppermute(array, 'seq', pairs)  28.1 us
    pallas_call x2, Pallas kernels, attend(): pl.pallas_call(functools.partial(attend_kernel, n=n), out_shape=tuple((ja...  9.41 us
    unnamed x26, local copies, waits for them, and re-layouts  6.53 us
    pallas_call x1, Pallas kernels, rope_packs(): pl.pallas_call(functools.partial(rope_kernel, n=n, sizes=sizes), out_shap...  3.36 us
  transfers between devices with their start and end apart: 17, of which 5 were waited for; matrix products, arithmetic and copies ran while one was open for 0% of the time, Pallas kernels for 13%

profile of v2, /device:TPU:0, one launch (start us, length us, event | category | flops | bytes accessed | tf_op | source)
XLA Modules:
  0.0 102.7 jit_solution(2842763666503458842)
XLA Ops:
  0.6 0.0 copy-start.2
  0.6 0.0 copy-start.1
  0.6 2.0 %pack_values.1 = (bf16[1,128,512]{2,1,0:T(8,128)(2,1)S(1)}, bf16[2,128,512]{2,1,0:T(8,128)(2,1)}, bf16[2,128,512]{2,1,0:T(8,128)(2,1)S(1)}) custom-call(bf16[1,128,2048]{2,1,0:T(8,128)(2,1)} %v_ref.5, bf16[1,128,2048]{2,1,0:T(8,128)(2,1)} %vd_ref.3), custom_call_target="tpu_custom_call" | custom-call | bytes 1310720 | tf_op jit(solution)/shard_map/pack_values/pallas_call | solution.py:70
  2.6 3.1 %collective-permute-start.3 = (bf16[2,128,512]{2,1,0:T(8,128)(2,1)}, bf16[2,128,512]{2,1,0:T(8,128)(2,1)S(1)}, u32[]{:S(2)}, u32[]{:S(2)}) collective-permute-start(bf16[2,128,512]{2,1,0:T(8,128)(2,1)} %get-tuple-element.27), channel_id=1, source_target_pairs={{1,0},{0,1},{3,2},{2,3},{5,4},{4,5},{7,6},{6,7},{9,8},{8,9},{11,10... | collective-permute-start | bytes 786440 | tf_op jit(solution)/shard_map/ppermute | solution.py:283
  5.8 2.6 %collective-permute-start.4 = (bf16[2,128,512]{2,1,0:T(8,128)(2,1)S(1)}, bf16[2,128,512]{2,1,0:T(8,128)(2,1)S(1)}, u32[]{:S(2)}, u32[]{:S(2)}) collective-permute-start(bf16[2,128,512]{2,1,0:T(8,128)(2,1)S(1)} %get-tuple-element.28), channel_id=1, source_target_pairs={{2,0},{3,1},{0,2},{1,3},{6,4},{7,5},{4,6},{5,7},{10,8},{11,9},{8,1... | collective-permute-start | bytes 786440 | tf_op jit(solution)/shard_map/ppermute | solution.py:283
  9.1 0.3 fusion
  9.4 0.0 copy-done.2
  9.5 0.0 copy-done.1
  9.5 0.0 copy-start.3
  9.5 1.0 %copy-done.3 = bf16[1,128,2048]{2,1,0:T(8,128)(2,1)S(1)} copy-done((bf16[1,128,2048]{2,1,0:T(8,128)(2,1)S(1)}, bf16[1,128,2048]{2,1,0:T(8,128)(2,1)}, u32[]{:S(2)}) %copy-start.3) | copy-done | bytes 524312
  10.5 1.0 %copy-done.4 = bf16[1,128,2048]{2,1,0:T(8,128)(2,1)S(1)} copy-done((bf16[1,128,2048]{2,1,0:T(8,128)(2,1)S(1)}, bf16[1,128,2048]{2,1,0:T(8,128)(2,1)}, u32[]{:S(2)}) %copy-start.4) | copy-done | bytes 524312
  11.6 0.0 copy-start
  11.6 0.0 copy-start.5
  11.6 3.4 %rope_packs.1 = (bf16[4,128,256]{2,1,0:T(8,128)(2,1)S(1)}, bf16[4,128,256]{2,1,0:T(8,128)(2,1)}, bf16[4,128,256]{2,1,0:T(8,128)(2,1)S(1)}, bf16[4,128,256]{2,1,0...) custom-call(s32[4]{0:T(128)S(1)} %iota_xor_fusion.blk_ref, ...), custom_call_target="tpu_custom_call" | custom-call | flops 6291456 | bytes 4194304 | tf_op jit(solution)/shard_map/rope_packs/pallas_call | solution.py:116
  14.9 0.0 copy-start.6
  14.9 0.7 copy-done.6
  15.6 0.0 copy-start.8
  15.6 0.7 copy-done.8
  16.3 0.0 copy-start.9
  16.3 0.7 copy-done.9
  17.0 0.0 copy-start.11
  17.0 0.7 copy-done.11
  17.7 0.0 copy-start.12
  17.7 0.7 copy-done.12
  18.4 0.4 collective-permute-start.11
  18.9 0.0 copy-done
  18.9 1.4 %collective-permute-start.5 = (bf16[1,128,512]{2,1,0:T(8,128)(2,1)S(1)}, bf16[1,128,512]{2,1,0:T(8,128)(2,1)S(1)}, u32[]{:S(2)}, u32[]{:S(2)}) collective-permute-start(bf16[1,128,512]{2,1,0:T(8,128)(2,1)S(1)} %constant_dynamic-slice_fusion), channel_id=1, source_target_pairs={{3,0},{2,1},{1,2},{0,3},{7,4},{6,5},{5,6},{4,7},{11,8},{10,9},{9,1... | collective-permute-start | bytes 393224 | tf_op jit(solution)/shard_map/ppermute | solution.py:283
  20.3 2.5 %collective-permute-start.6 = (bf16[1,128,512]{2,1,0:T(8,128)(2,1)S(1)}, bf16[1,128,512]{2,1,0:T(8,128)(2,1)S(1)}, u32[]{:S(2)}, u32[]{:S(2)}) collective-permute-start(bf16[1,128,512]{2,1,0:T(8,128)(2,1)S(1)} %get-tuple-element.29), channel_id=1, source_target_pairs={{3,0},{2,1},{1,2},{0,3},{7,4},{6,5},{5,6},{4,7},{11,8},{10,9},{9,1... | collective-permute-start | bytes 393224 | tf_op jit(solution)/shard_map/ppermute | solution.py:283
  22.8 7.4 %collective-permute-done.5.refs_6_ = bf16[1,128,512]{2,1,0:T(8,128)(2,1)S(1)} collective-permute-done((bf16[1,128,512]{2,1,0:T(8,128)(2,1)S(1)}, bf16[1,128,512]{2,1,0:T(8,128)(2,1)S(1)}, u32[]{:S(2)}, u32[]{:S(2)}) %collective-permute-start.5) | collective-permute-done | bytes 131104 | tf_op jit(solution)/shard_map/ppermute | solution.py:283
  30.2 0.0 collective-permute-start.12
  30.2 2.6 %collective-permute-done.6.refs_7_ = bf16[1,128,512]{2,1,0:T(8,128)(2,1)S(1)} collective-permute-done((bf16[1,128,512]{2,1,0:T(8,128)(2,1)S(1)}, bf16[1,128,512]{2,1,0:T(8,128)(2,1)S(1)}, u32[]{:S(2)}, u32[]{:S(2)}) %collective-permute-start.6) | collective-permute-done | bytes 131104 | tf_op jit(solution)/shard_map/ppermute | solution.py:283
  32.8 3.0 %collective-permute-start.13 = (bf16[4,128,256]{2,1,0:T(8,128)(2,1)}, bf16[4,128,256]{2,1,0:T(8,128)(2,1)S(1)}, u32[]{:S(2)}, u32[]{:S(2)}) collective-permute-start(bf16[4,128,256]{2,1,0:T(8,128)(2,1)} %copy-done.11), channel_id=1, source_target_pairs={{3,0},{2,1},{1,2},{0,3},{7,4},{6,5},{5,6},{4,7},{11,8},{10,9},{9,1... | collective-permute-start | bytes 786440 | tf_op jit(solution)/shard_map/ppermute | solution.py:283
  35.8 0.0 collective-permute-done.3.refs_4_
  35.8 9.3 %collective-permute-start = (bf16[4,128,256]{2,1,0:T(8,128)(2,1)}, bf16[4,128,256]{2,1,0:T(8,128)(2,1)S(1)}, u32[]{:S(2)}, u32[]{:S(2)}) collective-permute-start(bf16[4,128,256]{2,1,0:T(8,128)(2,1)} %copy-done.8), channel_id=1, source_target_pairs={{1,0},{0,1},{3,2},{2,3},{5,4},{4,5},{7,6},{6,7},{9,8},{8,9},{11,10... | collective-permute-start | bytes 786440 | tf_op jit(solution)/shard_map/ppermute | solution.py:283
  45.1 0.0 collective-permute-done.4.refs_5_
  45.1 0.0 copy-done.7
  45.1 1.5 %collective-permute-start.1 = (bf16[4,128,256]{2,1,0:T(8,128)(2,1)S(1)}, bf16[4,128,256]{2,1,0:T(8,128)(2,1)S(1)}, u32[]{:S(2)}, u32[]{:S(2)}) collective-permute-start(bf16[4,128,256]{2,1,0:T(8,128)(2,1)S(1)} %copy-done.7), channel_id=1, source_target_pairs={{2,0},{3,1},{0,2},{1,3},{6,4},{7,5},{4,6},{5,7},{10,8},{11,9},{8,1... | collective-permute-start | bytes 786440 | tf_op jit(solution)/shard_map/ppermute | solution.py:283
  46.6 0.0 collective-permute-done.11.refs_1_
  46.6 1.5 %collective-permute-start.2 = (bf16[4,128,256]{2,1,0:T(8,128)(2,1)S(1)}, bf16[4,128,256]{2,1,0:T(8,128)(2,1)S(1)}, u32[]{:S(2)}, u32[]{:S(2)}) collective-permute-start(bf16[4,128,256]{2,1,0:T(8,128)(2,1)S(1)} %get-tuple-element.26), channel_id=1, source_target_pairs={{3,0},{2,1},{1,2},{0,3},{7,4},{6,5},{5,6},{4,7},{11,8},{10,9},{9,1... | collective-permute-start | bytes 786440 | tf_op jit(solution)/shard_map/ppermute | solution.py:283
  48.1 14.0 %collective-permute-done.12.refs_2_ = bf16[4,128,256]{2,1,0:T(8,128)(2,1)S(1)} collective-permute-done((bf16[4,128,256]{2,1,0:T(8,128)(2,1)}, bf16[4,128,256]{2,1,0:T(8,128)(2,1)S(1)}, u32[]{:S(2)}, u32[]{:S(2)}) %collective-permute-start.12) | collective-permute-done | bytes 262176 | tf_op jit(solution)/shard_map/ppermute | solution.py:283
  62.1 0.0 collective-permute-done.13.refs_3_
  62.1 0.0 copy-done.5
  62.1 0.9 copy-done.10
  63.1 4.7 %attend.3 = (bf16[2,128,256]{2,1,0:T(8,128)(2,1)S(1)}, bf16[2,128,256]{2,1,0:T(8,128)(2,1)S(1)}, bf16[2,128,256]{2,1,0:T(8,128)(2,1)S(1)}, bf16[2,128,256]{2,1,0:T(8,128)(2,1)S(1)}) custom-call(s32[4]{0:T(128)S(1)} %iota_xor_fusion.blk_ref, bf16[1,128,2048]{2,1,0:T(8,128)(2,1)S(1)} %copy-done, bf16[1,128,2048]{2,1,0:T(8,128)(2,1)S(1)} %copy-done.5, ...), custom_call_target="tpu_custom_call" | custom-call | flops 805306368 | bytes 2097152 | tf_op jit(solution)/shard_map/attend/pallas_call | solution.py:187
  67.7 0.2 collective-permute-start.14
  67.9 8.9 %collective-permute-start.15 = (bf16[2,128,256]{2,1,0:T(8,128)(2,1)S(1)}, bf16[2,128,256]{2,1,0:T(8,128)(2,1)S(1)}, u32[]{:S(2)}, u32[]{:S(2)}) collective-permute-start(bf16[2,128,256]{2,1,0:T(8,128)(2,1)S(1)} %get-tuple-element.39), channel_id=1, source_target_pairs={{2,0},{3,1},{0,2},{1,3},{6,4},{7,5},{4,6},{5,7},{10,8},{11,9},{8,1... | collective-permute-start | bytes 393224 | tf_op jit(solution)/shard_map/ppermute | solution.py:283
  76.8 0.0 collective-permute-done.refs_1_
  76.9 0.0 collective-permute-done.1.refs_2_
  76.9 0.0 collective-permute-done.2.refs_3_
  76.9 4.7 %attend.2 = (bf16[2,128,256]{2,1,0:T(8,128)(2,1)S(1)}, bf16[2,128,256]{2,1,0:T(8,128)(2,1)S(1)}, bf16[2,128,256]{2,1,0:T(8,128)(2,1)S(1)}, bf16[2,128,256]{2,1,0:T(8,128)(2,1)S(1)}) custom-call(s32[4]{0:T(128)S(1)} %iota_xor_fusion.blk_ref, bf16[1,128,2048]{2,1,0:T(8,128)(2,1)S(1)} %copy-done, bf16[1,128,2048]{2,1,0:T(8,128)(2,1)S(1)} %copy-done.5, ...), custom_call_target="tpu_custom_call" | custom-call | flops 805306368 | bytes 2097152 | tf_op jit(solution)/shard_map/attend/pallas_call | solution.py:187
  81.6 7.3 %collective-permute-start.8 = (bf16[2,128,256]{2,1,0:T(8,128)(2,1)S(1)}, bf16[2,128,256]{2,1,0:T(8,128)(2,1)S(1)}, u32[]{:S(2)}, u32[]{:S(2)}) collective-permute-start(bf16[2,128,256]{2,1,0:T(8,128)(2,1)S(1)} %get-tuple-element.31), channel_id=1, source_target_pairs={{2,0},{3,1},{0,2},{1,3},{6,4},{7,5},{4,6},{5,7},{10,8},{11,9},{8,1... | collective-permute-start | bytes 393224 | tf_op jit(solution)/shard_map/ppermute | solution.py:283
  88.9 1.1 %collective-permute-start.16 = (bf16[2,128,256]{2,1,0:T(8,128)(2,1)S(1)}, bf16[2,128,256]{2,1,0:T(8,128)(2,1)S(1)}, u32[]{:S(2)}, u32[]{:S(2)}) collective-permute-start(bf16[2,128,256]{2,1,0:T(8,128)(2,1)S(1)} %get-tuple-element.40), channel_id=1, source_target_pairs={{1,0},{0,1},{3,2},{2,3},{5,4},{4,5},{7,6},{6,7},{9,8},{8,9},{11,10... | collective-permute-start | bytes 393224 | tf_op jit(solution)/shard_map/ppermute | solution.py:283
  90.0 0.9 collective-permute-start.9
  90.9 0.0 collective-permute-done.14.refs_1_
  90.9 0.7 collective-permute-start.10
  91.6 0.0 collective-permute-done.15.refs_2_
  91.6 5.3 %collective-permute-start.7 = (bf16[2,128,256]{2,1,0:T(8,128)(2,1)S(1)}, bf16[2,128,256]{2,1,0:T(8,128)(2,1)S(1)}, u32[]{:S(2)}, u32[]{:S(2)}) collective-permute-start(bf16[2,128,256]{2,1,0:T(8,128)(2,1)S(1)} %get-tuple-element.30), channel_id=1, source_target_pairs={{3,0},{0,3},{7,4},{4,7},{11,8},{8,11},{15,12},{12,15},{19,16},{16,... | collective-permute-start | bytes 393224 | tf_op jit(solution)/shard_map/ppermute | solution.py:283
  96.9 0.0 collective-permute-done.16.refs_3_
  96.9 0.9 place.2
  97.8 0.0 collective-permute-done.8.refs_1_
  97.9 1.5 %collective-permute-done.9.refs_2_ = bf16[2,128,256]{2,1,0:T(8,128)(2,1)S(1)} collective-permute-done((bf16[2,128,256]{2,1,0:T(8,128)(2,1)S(1)}, bf16[2,128,256]{2,1,0:T(8,128)(2,1)S(1)}, u32[]{:S(2)}, u32[]{:S(2)}) %collective-permute-start.9) | collective-permute-done | bytes 131104 | tf_op jit(solution)/shard_map/ppermute | solution.py:283
  99.3 0.0 collective-permute-done.10.refs_3_
  99.3 2.5 %collective-permute-done.7.refs_0_ = bf16[2,128,256]{2,1,0:T(8,128)(2,1)S(1)} collective-permute-done((bf16[2,128,256]{2,1,0:T(8,128)(2,1)S(1)}, bf16[2,128,256]{2,1,0:T(8,128)(2,1)S(1)}, u32[]{:S(2)}, u32[]{:S(2)}) %collective-permute-start.7) | collective-permute-done | bytes 131104 | tf_op jit(solution)/shard_map/ppermute | solution.py:283
  101.9 0.8 place.3
  (9 shorter events, 0.1 us)
Async XLA Ops:
  0.6 8.8 %copy-start.2 = (bf16[1,128,2048]{2,1,0:T(8,128)(2,1)S(1)}, bf16[1,128,2048]{2,1,0:T(8,128)(2,1)}, u32[]{:S(2)}) copy-start(bf16[1,128,2048]{2,1,0:T(8,128)(2,1)} %k_ref.1) | copy-start | bytes 1572868
  0.6 8.8 %copy-start.1 = (bf16[1,128,2048]{2,1,0:T(8,128)(2,1)S(1)}, bf16[1,128,2048]{2,1,0:T(8,128)(2,1)}, u32[]{:S(2)}) copy-start(bf16[1,128,2048]{2,1,0:T(8,128)(2,1)} %q_ref.1) | copy-start | bytes 1572868
  2.6 33.1 %collective-permute-start.3 = (bf16[2,128,512]{2,1,0:T(8,128)(2,1)}, bf16[2,128,512]{2,1,0:T(8,128)(2,1)S(1)}, u32[]{:S(2)}, u32[]{:S(2)}) collective-permute-start(bf16[2,128,512]{2,1,0:T(8,128)(2,1)} %get-tuple-element.27), channel_id=1, source_target_pairs={{1,0},{0,1},{3,2},{2,3},{5,4},{4,5},{7,6},{6,7},{9,8},{8,9},{11,10... | collective-permute-start | bytes 786440 | tf_op jit(solution)/shard_map/ppermute | solution.py:283
  5.8 39.3 %collective-permute-start.4 = (bf16[2,128,512]{2,1,0:T(8,128)(2,1)S(1)}, bf16[2,128,512]{2,1,0:T(8,128)(2,1)S(1)}, u32[]{:S(2)}, u32[]{:S(2)}) collective-permute-start(bf16[2,128,512]{2,1,0:T(8,128)(2,1)S(1)} %get-tuple-element.28), channel_id=1, source_target_pairs={{2,0},{3,1},{0,2},{1,3},{6,4},{7,5},{4,6},{5,7},{10,8},{11,9},{8,1... | collective-permute-start | bytes 786440 | tf_op jit(solution)/shard_map/ppermute | solution.py:283
  9.5 1.0 %copy-start.3 = (bf16[1,128,2048]{2,1,0:T(8,128)(2,1)S(1)}, bf16[1,128,2048]{2,1,0:T(8,128)(2,1)}, u32[]{:S(2)}) copy-start(bf16[1,128,2048]{2,1,0:T(8,128)(2,1)} %qd_ref.1) | copy-start | bytes 1572868
  10.5 1.0 %copy-start.4 = (bf16[1,128,2048]{2,1,0:T(8,128)(2,1)S(1)}, bf16[1,128,2048]{2,1,0:T(8,128)(2,1)}, u32[]{:S(2)}) copy-start(bf16[1,128,2048]{2,1,0:T(8,128)(2,1)} %kd_ref.1) | copy-start | bytes 1572868
  11.6 7.3 %copy-start = (bf16[1,128,2048]{2,1,0:T(8,128)(2,1)S(1)}, bf16[1,128,2048]{2,1,0:T(8,128)(2,1)}, u32[]{:S(2)}) copy-start(bf16[1,128,2048]{2,1,0:T(8,128)(2,1)} %v_ref.5) | copy-start | bytes 1572868
  11.6 50.5 %copy-start.5 = (bf16[1,128,2048]{2,1,0:T(8,128)(2,1)S(1)}, bf16[1,128,2048]{2,1,0:T(8,128)(2,1)}, u32[]{:S(2)}) copy-start(bf16[1,128,2048]{2,1,0:T(8,128)(2,1)} %vd_ref.3) | copy-start | bytes 1572868
  14.9 0.7 copy-start.6
  15.6 0.7 copy-start.8
  16.3 0.7 copy-start.9
  17.0 0.7 copy-start.11
  17.7 0.7 copy-start.12
  18.4 26.7 %copy-start.7 = (bf16[4,128,256]{2,1,0:T(8,128)(2,1)S(1)}, bf16[4,128,256]{2,1,0:T(8,128)(2,1)}, u32[]{:S(2)}) copy-start(bf16[4,128,256]{2,1,0:T(8,128)(2,1)} %copy-done.6) | copy-start | bytes 786436
  18.4 28.2 %collective-permute-start.11 = (bf16[4,128,256]{2,1,0:T(8,128)(2,1)}, bf16[4,128,256]{2,1,0:T(8,128)(2,1)S(1)}, u32[]{:S(2)}, u32[]{:S(2)}) collective-permute-start(bf16[4,128,256]{2,1,0:T(8,128)(2,1)} %get-tuple-element.34), channel_id=1, source_target_pairs={{1,0},{0,1},{3,2},{2,3},{5,4},{4,5},{7,6},{6,7},{9,8},{8,9},{11,10... | collective-permute-start | bytes 786440 | tf_op jit(solution)/shard_map/ppermute | solution.py:283
  18.9 11.3 %collective-permute-start.5 = (bf16[1,128,512]{2,1,0:T(8,128)(2,1)S(1)}, bf16[1,128,512]{2,1,0:T(8,128)(2,1)S(1)}, u32[]{:S(2)}, u32[]{:S(2)}) collective-permute-start(bf16[1,128,512]{2,1,0:T(8,128)(2,1)S(1)} %constant_dynamic-slice_fusion), channel_id=1, source_target_pairs={{3,0},{2,1},{1,2},{0,3},{7,4},{6,5},{5,6},{4,7},{11,8},{10,9},{9,1... | collective-permute-start | bytes 393224 | tf_op jit(solution)/shard_map/ppermute | solution.py:283
  20.3 12.5 %collective-permute-start.6 = (bf16[1,128,512]{2,1,0:T(8,128)(2,1)S(1)}, bf16[1,128,512]{2,1,0:T(8,128)(2,1)S(1)}, u32[]{:S(2)}, u32[]{:S(2)}) collective-permute-start(bf16[1,128,512]{2,1,0:T(8,128)(2,1)S(1)} %get-tuple-element.29), channel_id=1, source_target_pairs={{3,0},{2,1},{1,2},{0,3},{7,4},{6,5},{5,6},{4,7},{11,8},{10,9},{9,1... | collective-permute-start | bytes 393224 | tf_op jit(solution)/shard_map/ppermute | solution.py:283
  30.2 31.9 %collective-permute-start.12 = (bf16[4,128,256]{2,1,0:T(8,128)(2,1)}, bf16[4,128,256]{2,1,0:T(8,128)(2,1)S(1)}, u32[]{:S(2)}, u32[]{:S(2)}) collective-permute-start(bf16[4,128,256]{2,1,0:T(8,128)(2,1)} %copy-done.12), channel_id=1, source_target_pairs={{2,0},{3,1},{0,2},{1,3},{6,4},{7,5},{4,6},{5,7},{10,8},{11,9},{8,1... | collective-permute-start | bytes 786440 | tf_op jit(solution)/shard_map/ppermute | solution.py:283
  32.8 29.3 %collective-permute-start.13 = (bf16[4,128,256]{2,1,0:T(8,128)(2,1)}, bf16[4,128,256]{2,1,0:T(8,128)(2,1)S(1)}, u32[]{:S(2)}, u32[]{:S(2)}) collective-permute-start(bf16[4,128,256]{2,1,0:T(8,128)(2,1)} %copy-done.11), channel_id=1, source_target_pairs={{3,0},{2,1},{1,2},{0,3},{7,4},{6,5},{5,6},{4,7},{11,8},{10,9},{9,1... | collective-permute-start | bytes 786440 | tf_op jit(solution)/shard_map/ppermute | solution.py:283
  35.8 41.1 %collective-permute-start = (bf16[4,128,256]{2,1,0:T(8,128)(2,1)}, bf16[4,128,256]{2,1,0:T(8,128)(2,1)S(1)}, u32[]{:S(2)}, u32[]{:S(2)}) collective-permute-start(bf16[4,128,256]{2,1,0:T(8,128)(2,1)} %copy-done.8), channel_id=1, source_target_pairs={{1,0},{0,1},{3,2},{2,3},{5,4},{4,5},{7,6},{6,7},{9,8},{8,9},{11,10... | collective-permute-start | bytes 786440 | tf_op jit(solution)/shard_map/ppermute | solution.py:283
  45.1 31.8 %collective-permute-start.1 = (bf16[4,128,256]{2,1,0:T(8,128)(2,1)S(1)}, bf16[4,128,256]{2,1,0:T(8,128)(2,1)S(1)}, u32[]{:S(2)}, u32[]{:S(2)}) collective-permute-start(bf16[4,128,256]{2,1,0:T(8,128)(2,1)S(1)} %copy-done.7), channel_id=1, source_target_pairs={{2,0},{3,1},{0,2},{1,3},{6,4},{7,5},{4,6},{5,7},{10,8},{11,9},{8,1... | collective-permute-start | bytes 786440 | tf_op jit(solution)/shard_map/ppermute | solution.py:283
  46.6 30.2 %collective-permute-start.2 = (bf16[4,128,256]{2,1,0:T(8,128)(2,1)S(1)}, bf16[4,128,256]{2,1,0:T(8,128)(2,1)S(1)}, u32[]{:S(2)}, u32[]{:S(2)}) collective-permute-start(bf16[4,128,256]{2,1,0:T(8,128)(2,1)S(1)} %get-tuple-element.26), channel_id=1, source_target_pairs={{3,0},{2,1},{1,2},{0,3},{7,4},{6,5},{5,6},{4,7},{11,8},{10,9},{9,1... | collective-permute-start | bytes 786440 | tf_op jit(solution)/shard_map/ppermute | solution.py:283
  62.1 1.0 copy-start.10
  67.7 23.2 %collective-permute-start.14 = (bf16[2,128,256]{2,1,0:T(8,128)(2,1)S(1)}, bf16[2,128,256]{2,1,0:T(8,128)(2,1)S(1)}, u32[]{:S(2)}, u32[]{:S(2)}) collective-permute-start(bf16[2,128,256]{2,1,0:T(8,128)(2,1)S(1)} %get-tuple-element.38), channel_id=1, source_target_pairs={{3,0},{2,1},{1,2},{0,3},{7,4},{6,5},{5,6},{4,7},{11,8},{10,9},{9,1... | collective-permute-start | bytes 393224 | tf_op jit(solution)/shard_map/ppermute | solution.py:283
  67.9 23.7 %collective-permute-start.15 = (bf16[2,128,256]{2,1,0:T(8,128)(2,1)S(1)}, bf16[2,128,256]{2,1,0:T(8,128)(2,1)S(1)}, u32[]{:S(2)}, u32[]{:S(2)}) collective-permute-start(bf16[2,128,256]{2,1,0:T(8,128)(2,1)S(1)} %get-tuple-element.39), channel_id=1, source_target_pairs={{2,0},{3,1},{0,2},{1,3},{6,4},{7,5},{4,6},{5,7},{10,8},{11,9},{8,1... | collective-permute-start | bytes 393224 | tf_op jit(solution)/shard_map/ppermute | solution.py:283
  81.6 16.2 %collective-permute-start.8 = (bf16[2,128,256]{2,1,0:T(8,128)(2,1)S(1)}, bf16[2,128,256]{2,1,0:T(8,128)(2,1)S(1)}, u32[]{:S(2)}, u32[]{:S(2)}) collective-permute-start(bf16[2,128,256]{2,1,0:T(8,128)(2,1)S(1)} %get-tuple-element.31), channel_id=1, source_target_pairs={{2,0},{3,1},{0,2},{1,3},{6,4},{7,5},{4,6},{5,7},{10,8},{11,9},{8,1... | collective-permute-start | bytes 393224 | tf_op jit(solution)/shard_map/ppermute | solution.py:283
  88.9 8.0 %collective-permute-start.16 = (bf16[2,128,256]{2,1,0:T(8,128)(2,1)S(1)}, bf16[2,128,256]{2,1,0:T(8,128)(2,1)S(1)}, u32[]{:S(2)}, u32[]{:S(2)}) collective-permute-start(bf16[2,128,256]{2,1,0:T(8,128)(2,1)S(1)} %get-tuple-element.40), channel_id=1, source_target_pairs={{1,0},{0,1},{3,2},{2,3},{5,4},{4,5},{7,6},{6,7},{9,8},{8,9},{11,10... | collective-permute-start | bytes 393224 | tf_op jit(solution)/shard_map/ppermute | solution.py:283
  90.0 9.3 %collective-permute-start.9 = (bf16[2,128,256]{2,1,0:T(8,128)(2,1)S(1)}, bf16[2,128,256]{2,1,0:T(8,128)(2,1)S(1)}, u32[]{:S(2)}, u32[]{:S(2)}) collective-permute-start(bf16[2,128,256]{2,1,0:T(8,128)(2,1)S(1)} %get-tuple-element.32), channel_id=1, source_target_pairs={{1,0},{0,1},{3,2},{2,3},{5,4},{4,5},{7,6},{6,7},{9,8},{8,9},{11,10... | collective-permute-start | bytes 393224 | tf_op jit(solution)/shard_map/ppermute | solution.py:283
  90.9 8.4 %collective-permute-start.10 = (bf16[2,128,256]{2,1,0:T(8,128)(2,1)S(1)}, bf16[2,128,256]{2,1,0:T(8,128)(2,1)S(1)}, u32[]{:S(2)}, u32[]{:S(2)}) collective-permute-start(bf16[2,128,256]{2,1,0:T(8,128)(2,1)S(1)} %get-tuple-element.30), channel_id=1, source_target_pairs={{2,1},{1,2},{6,5},{5,6},{10,9},{9,10},{14,13},{13,14},{18,17},{17,... | collective-permute-start | bytes 393224 | tf_op jit(solution)/shard_map/ppermute | solution.py:283
  91.6 10.3 %collective-permute-start.7 = (bf16[2,128,256]{2,1,0:T(8,128)(2,1)S(1)}, bf16[2,128,256]{2,1,0:T(8,128)(2,1)S(1)}, u32[]{:S(2)}, u32[]{:S(2)}) collective-permute-start(bf16[2,128,256]{2,1,0:T(8,128)(2,1)S(1)} %get-tuple-element.30), channel_id=1, source_target_pairs={{3,0},{0,3},{7,4},{4,7},{11,8},{8,11},{15,12},{12,15},{19,16},{16,... | collective-permute-start | bytes 393224 | tf_op jit(solution)/shard_map/ppermute | solution.py:283
